TPU v7x, 128 devices: a whole 4x4x4 slice. The times are simulated.
128 devices in a mesh: stripe: 32 (over x, y_lo, z), sub: 4 (over y_hi, core).
Axes of the slice: x: 4, y: 4 (y_hi: 2, y_lo: 2; y = y_hi * 2 + y_lo), z: 4, core: 2. Of those that a mesh axis runs over, the one named last changes fastest.
Arguments:
- channel: float32 [8, 32, 64, 512], P('sub', 'stripe'), may hold values from -0.25 to 0.25
- received: float32 [8, 32, 2048], P('sub', None, 'stripe'), may hold values from -18 to 18
- noise_var: float32 [8, 32], P('sub', 'stripe'), may hold values from 0.25 to 4
- downlink: float32 [8, 32, 512], P('sub'), may hold values from -6 to 6
- user_order: int32 [512], P('stripe'), may hold values from 0 to 511, each once
Outputs:
- transmit: float32 [8, 32, 2048], P('sub', None, 'stripe')
- owned: float32 [8, 32, 512], P('sub', None, 'stripe')
Inputs may be any that keep to these rules, and one draw needn't show every extreme that they name: `user_order`: a permutation of the 512 users.
All inputs are finite; a program needn't handle non-finite values.
Results may differ from a plain program's by a relative error of at most 0.00017.
Values sent between devices are 32-bit elements; how exact they have to be, the bound alone decides.
No kernel may reach another device: no remote copies, remote signals or barrier semaphores. Data moves between devices by JAX's collectives and lax.ppermute only.
A program may use at most 256 MiB of HBM per device.

v0:
```python
import jax
import jax.numpy as jnp
from jax import lax
from jax.sharding import PartitionSpec as P

prior_var = 0.1


def from_behind(value, axis, steps):
    count = lax.axis_size(axis)
    first, last = (max(0, -steps), min(count, count - steps))
    return lax.ppermute(value, axis, [(source, source + steps) for source in range(first, last)])


def from_root(block, axis, source):
    block = jnp.where(lax.axis_index(axis) == source, block, jnp.zeros_like(block))
    return lax.psum(block, axis)


def product(left, right):
    return jnp.dot(left, right, precision=lax.Precision.HIGHEST, preferred_element_type=jnp.float32)


def woodbury(covariance, estimate, matrix, samples, variance):
    cross_term = product(covariance, matrix.T)
    system = product(matrix, cross_term) + variance * jnp.eye(matrix.shape[0], dtype=jnp.float32)
    factor = jnp.linalg.cholesky(system)
    gain_rows = jax.scipy.linalg.cho_solve((factor, True), cross_term.T)
    residual_rows = samples - product(estimate, matrix.T)
    estimate = estimate + product(residual_rows, gain_rows)
    covariance = covariance - product(cross_term, gain_rows)
    return (covariance, estimate)


def shards(channel, received, noise_var, downlink, user_order):
    local_blocks, local_links, antennas, user_count = channel.shape
    symbols = received.shape[1]
    samples = received.reshape(local_blocks, symbols, local_links, antennas).transpose(0, 2, 1, 3)
    eye_users = jnp.eye(user_count, dtype=jnp.float32)
    position = lax.axis_index("stripe")
    length = lax.axis_size("stripe")
    prior_cov = prior_var * eye_users
    prior_est = jnp.zeros((symbols, user_count), jnp.float32)

    def apply_links(covariance, estimate, block_index):
        matrices = lax.dynamic_index_in_dim(channel, block_index, 0, keepdims=False)
        sample_rows = lax.dynamic_index_in_dim(samples, block_index, 0, keepdims=False)
        variances = lax.dynamic_index_in_dim(noise_var, block_index, 0, keepdims=False)
        covariance, estimate = woodbury(
            covariance, estimate, matrices[0], sample_rows[0], variances[0]
        )
        return (covariance, estimate)

    def one_turn(turn_index, carried):
        out_cov, out_est, kept_cov, kept_est = carried
        in_cov, in_est = from_behind((out_cov, out_est), "stripe", 1)
        is_first = position == 0
        in_cov = jnp.where(is_first, prior_cov, in_cov)
        in_est = jnp.where(is_first, prior_est, in_est)
        block_index = turn_index - position
        is_valid = (block_index >= 0) & (block_index < local_blocks)
        clipped = jnp.clip(block_index, 0, local_blocks - 1)
        new_cov, new_est = apply_links(in_cov, in_est, clipped)
        keep_it = is_valid & (position == length - 1)
        old_cov = lax.dynamic_index_in_dim(kept_cov, clipped, 0, keepdims=False)
        old_est = lax.dynamic_index_in_dim(kept_est, clipped, 0, keepdims=False)
        kept_cov = lax.dynamic_update_index_in_dim(
            kept_cov, jnp.where(keep_it, new_cov, old_cov), clipped, 0
        )
        kept_est = lax.dynamic_update_index_in_dim(
            kept_est, jnp.where(keep_it, new_est, old_est), clipped, 0
        )
        return (new_cov, new_est, kept_cov, kept_est)

    initial = (
        prior_cov,
        prior_est,
        jnp.zeros((local_blocks, user_count, user_count), jnp.float32),
        jnp.zeros((local_blocks, symbols, user_count), jnp.float32),
    )
    carried = lax.fori_loop(0, local_blocks + length - 1, one_turn, initial)
    covars, estimates = (
        from_root(carried[2], "stripe", length - 1),
        from_root(carried[3], "stripe", length - 1),
    )
    diag_sum = jnp.sum(jnp.diagonal(covars, axis1=1, axis2=2), axis=0)
    total = lax.psum(diag_sum, "sub")
    mean_error = total / (local_blocks * lax.axis_size("sub"))
    power_scale = lax.rsqrt(mean_error)
    precoded = (
        jnp.einsum("bsk,bkn->bsn", downlink, covars, precision=lax.Precision.HIGHEST) * power_scale
    )
    transmit = jnp.einsum("bsk,blmk->bslm", precoded, channel, precision=lax.Precision.HIGHEST)
    transmit = transmit.reshape(local_blocks, symbols, local_links * antennas)
    owned_rows = jnp.take(estimates, user_order, axis=2)
    return (transmit, owned_rows)


def solution(mesh):
    return jax.shard_map(
        shards,
        mesh=mesh,
        in_specs=(
            P("sub", "stripe", None, None),
            P("sub", None, "stripe"),
            P("sub", "stripe"),
            P("sub", None, None),
            P("stripe"),
        ),
        out_specs=(P("sub", None, "stripe"), P("sub", None, "stripe")),
        check_vma=False,
    )
```

profile of v0, /device:TPU:1, one launch (start us, length us, event | category | flops | bytes accessed | tf_op | source)
XLA Modules:
  0.0 1959.1 jit_solution(15671876080877473592)
XLA Ops:
  9.3 1484.5 %while.21 = (s32[]{:T(128)}, f32[512,512]{1,0:T(8,128)}, f32[32,512]{1,0:T(8,128)S(1)}, f32[2,512,512]{2,1,0:T(8,128)S(1)}, f32[2,32,512]{2,1,0:T(8,128)}, /*ind...) while((s32[]{:T(128)}, f32[512,512]{1,0:T(8,128)}, ...), condition=%wide.region_3.4_spmd.clone, body=%wide.region_0.3_spmd.clone.sunk | while | flops 505559104 | bytes 14437732 | solution.py:81
  20.0 17.1 collective-permute-done.1
  71.3 16.3 collective-permute-done.1
  121.8 15.6 collective-permute-done.1
  171.6 14.8 collective-permute-done.1
  221.8 12.9 collective-permute-done.1
  272.3 10.1 collective-permute-done.1
  495.7 9.3 collective-permute-start
  931.9 10.1 collective-permute-start
  975.6 9.9 collective-permute-start
  1019.2 9.8 collective-permute-start
  1062.7 9.4 collective-permute-start
  1105.8 9.4 collective-permute-start
  1148.9 9.4 collective-permute-start
  1192.0 9.4 collective-permute-start
  1235.1 9.4 collective-permute-start
  1278.3 9.4 collective-permute-start
  1321.4 9.4 collective-permute-start
  1364.5 9.4 collective-permute-start
  1407.6 9.4 collective-permute-start
  1450.7 9.4 collective-permute-start
  1496.7 355.5 %all-reduce.3.cloned.1.call-done = (f32[2,512,512]{2,1,0:T(8,128)}, f32[2,32,512]{2,1,0:T(8,128)}) async-done(((f32[2,512,512]{2,1,0:T(8,128)}, f32[2,32,512]{2,1,0:T(8,128)}), (f32[2,512,512]{2,1,0:T(8,128)}, f32[2,32,512]{2,1,0:T(8,128)})) %all-reduce.3.cloned.1.call-update) | async-done | bytes 2228240 | tf_op jit(solution)/shard_map/psum | solution.py:17
  1854.7 60.2 %copy.23 = f32[2,512,512]{0,2,1:T(8,128)} copy(f32[2,512,512]{2,1,0:T(8,128)} %get-tuple-element.308) | data formatting | bytes 4194304 | tf_op jit(solution)/shard_map/psum | solution.py:17
  1920.6 28.3 %psum.22 = f32[512]{0:T(512)S(1)} all-reduce(f32[512]{0:T(512)S(1)} %reduce_sum.9), channel_id=1, replica_groups=mesh['stripe'=32,'sub'=4] {'sub'}, use_global_device_ids=true, to_apply=%region_6.7 | all-reduce | flops 512 | bytes 4096 | tf_op jit(solution)/shard_map/psum | solution.py:87
  (799 shorter events, 1277.5 us)
Async XLA Ops:
  7.2 1845.1 %all-reduce.3.cloned.1.call-start = ((), (), s32[]{:S(2)}) async-start(), calls=%async_computation | async-start | bytes 4456448 | tf_op jit(solution)/shard_map/psum | solution.py:17
  9.3 29.0 %collective-permute-start = (f32[512,512]{1,0:T(8,128)}, f32[512,512]{1,0:T(8,128)}, u32[]{:S(2)}, u32[]{:S(2)}) collective-permute-start(f32[512,512]{1,0:T(8,128)} %get-tuple-element.404), channel_id=1, source_target_pairs={{0,4},{4,8},{8,12},{12,16},{16,20},{20,24},{24,28},{28,32},{32,36}... | collective-permute-start | bytes 3145736 | tf_op jit(solution)/shard_map/while/body/eval_jaxpr/ppermute | solution.py:12
  14.7 22.4 %collective-permute-start.1 = (f32[32,512]{1,0:T(8,128)S(1)}, f32[32,512]{1,0:T(8,128)S(1)}, u32[]{:S(2)}, u32[]{:S(2)}) collective-permute-start(f32[32,512]{1,0:T(8,128)S(1)} %broadcast_select_fusion.4), channel_id=1, source_target_pairs={{0,4},{4,8},{8,12},{12,16},{16,20},{20,24},{24,28},{28,32},{32,36}... | collective-permute-start | bytes 196616 | tf_op jit(solution)/shard_map/while/body/eval_jaxpr/ppermute | solution.py:12
  59.2 29.6 %collective-permute-start = (f32[512,512]{1,0:T(8,128)}, f32[512,512]{1,0:T(8,128)}, u32[]{:S(2)}, u32[]{:S(2)}) collective-permute-start(f32[512,512]{1,0:T(8,128)} %get-tuple-element.404), channel_id=1, source_target_pairs={{0,4},{4,8},{8,12},{12,16},{16,20},{20,24},{24,28},{28,32},{32,36}... | collective-permute-start | bytes 3145736 | tf_op jit(solution)/shard_map/while/body/eval_jaxpr/ppermute | solution.py:12
  109.7 28.8 %collective-permute-start = (f32[512,512]{1,0:T(8,128)}, f32[512,512]{1,0:T(8,128)}, u32[]{:S(2)}, u32[]{:S(2)}) collective-permute-start(f32[512,512]{1,0:T(8,128)} %get-tuple-element.404), channel_id=1, source_target_pairs={{0,4},{4,8},{8,12},{12,16},{16,20},{20,24},{24,28},{28,32},{32,36}... | collective-permute-start | bytes 3145736 | tf_op jit(solution)/shard_map/while/body/eval_jaxpr/ppermute | solution.py:12
  159.5 28.1 %collective-permute-start = (f32[512,512]{1,0:T(8,128)}, f32[512,512]{1,0:T(8,128)}, u32[]{:S(2)}, u32[]{:S(2)}) collective-permute-start(f32[512,512]{1,0:T(8,128)} %get-tuple-element.404), channel_id=1, source_target_pairs={{0,4},{4,8},{8,12},{12,16},{16,20},{20,24},{24,28},{28,32},{32,36}... | collective-permute-start | bytes 3145736 | tf_op jit(solution)/shard_map/while/body/eval_jaxpr/ppermute | solution.py:12
  208.5 27.4 %collective-permute-start = (f32[512,512]{1,0:T(8,128)}, f32[512,512]{1,0:T(8,128)}, u32[]{:S(2)}, u32[]{:S(2)}) collective-permute-start(f32[512,512]{1,0:T(8,128)} %get-tuple-element.404), channel_id=1, source_target_pairs={{0,4},{4,8},{8,12},{12,16},{16,20},{20,24},{24,28},{28,32},{32,36}... | collective-permute-start | bytes 3145736 | tf_op jit(solution)/shard_map/while/body/eval_jaxpr/ppermute | solution.py:12
  256.8 26.7 %collective-permute-start = (f32[512,512]{1,0:T(8,128)}, f32[512,512]{1,0:T(8,128)}, u32[]{:S(2)}, u32[]{:S(2)}) collective-permute-start(f32[512,512]{1,0:T(8,128)} %get-tuple-element.404), channel_id=1, source_target_pairs={{0,4},{4,8},{8,12},{12,16},{16,20},{20,24},{24,28},{28,32},{32,36}... | collective-permute-start | bytes 3145736 | tf_op jit(solution)/shard_map/while/body/eval_jaxpr/ppermute | solution.py:12
  304.4 28.0 %collective-permute-start = (f32[512,512]{1,0:T(8,128)}, f32[512,512]{1,0:T(8,128)}, u32[]{:S(2)}, u32[]{:S(2)}) collective-permute-start(f32[512,512]{1,0:T(8,128)} %get-tuple-element.404), channel_id=1, source_target_pairs={{0,4},{4,8},{8,12},{12,16},{16,20},{20,24},{24,28},{28,32},{32,36}... | collective-permute-start | bytes 3145736 | tf_op jit(solution)/shard_map/while/body/eval_jaxpr/ppermute | solution.py:12
  353.4 27.3 %collective-permute-start = (f32[512,512]{1,0:T(8,128)}, f32[512,512]{1,0:T(8,128)}, u32[]{:S(2)}, u32[]{:S(2)}) collective-permute-start(f32[512,512]{1,0:T(8,128)} %get-tuple-element.404), channel_id=1, source_target_pairs={{0,4},{4,8},{8,12},{12,16},{16,20},{20,24},{24,28},{28,32},{32,36}... | collective-permute-start | bytes 3145736 | tf_op jit(solution)/shard_map/while/body/eval_jaxpr/ppermute | solution.py:12
  401.6 26.6 %collective-permute-start = (f32[512,512]{1,0:T(8,128)}, f32[512,512]{1,0:T(8,128)}, u32[]{:S(2)}, u32[]{:S(2)}) collective-permute-start(f32[512,512]{1,0:T(8,128)} %get-tuple-element.404), channel_id=1, source_target_pairs={{0,4},{4,8},{8,12},{12,16},{16,20},{20,24},{24,28},{28,32},{32,36}... | collective-permute-start | bytes 3145736 | tf_op jit(solution)/shard_map/while/body/eval_jaxpr/ppermute | solution.py:12
  449.1 25.6 %collective-permute-start = (f32[512,512]{1,0:T(8,128)}, f32[512,512]{1,0:T(8,128)}, u32[]{:S(2)}, u32[]{:S(2)}) collective-permute-start(f32[512,512]{1,0:T(8,128)} %get-tuple-element.404), channel_id=1, source_target_pairs={{0,4},{4,8},{8,12},{12,16},{16,20},{20,24},{24,28},{28,32},{32,36}... | collective-permute-start | bytes 3145736 | tf_op jit(solution)/shard_map/while/body/eval_jaxpr/ppermute | solution.py:12
  495.7 25.1 %collective-permute-start = (f32[512,512]{1,0:T(8,128)}, f32[512,512]{1,0:T(8,128)}, u32[]{:S(2)}, u32[]{:S(2)}) collective-permute-start(f32[512,512]{1,0:T(8,128)} %get-tuple-element.404), channel_id=1, source_target_pairs={{0,4},{4,8},{8,12},{12,16},{16,20},{20,24},{24,28},{28,32},{32,36}... | collective-permute-start | bytes 3145736 | tf_op jit(solution)/shard_map/while/body/eval_jaxpr/ppermute | solution.py:12
  541.7 24.4 %collective-permute-start = (f32[512,512]{1,0:T(8,128)}, f32[512,512]{1,0:T(8,128)}, u32[]{:S(2)}, u32[]{:S(2)}) collective-permute-start(f32[512,512]{1,0:T(8,128)} %get-tuple-element.404), channel_id=1, source_target_pairs={{0,4},{4,8},{8,12},{12,16},{16,20},{20,24},{24,28},{28,32},{32,36}... | collective-permute-start | bytes 3145736 | tf_op jit(solution)/shard_map/while/body/eval_jaxpr/ppermute | solution.py:12
  587.0 23.6 %collective-permute-start = (f32[512,512]{1,0:T(8,128)}, f32[512,512]{1,0:T(8,128)}, u32[]{:S(2)}, u32[]{:S(2)}) collective-permute-start(f32[512,512]{1,0:T(8,128)} %get-tuple-element.404), channel_id=1, source_target_pairs={{0,4},{4,8},{8,12},{12,16},{16,20},{20,24},{24,28},{28,32},{32,36}... | collective-permute-start | bytes 3145736 | tf_op jit(solution)/shard_map/while/body/eval_jaxpr/ppermute | solution.py:12
  631.6 22.7 %collective-permute-start = (f32[512,512]{1,0:T(8,128)}, f32[512,512]{1,0:T(8,128)}, u32[]{:S(2)}, u32[]{:S(2)}) collective-permute-start(f32[512,512]{1,0:T(8,128)} %get-tuple-element.404), channel_id=1, source_target_pairs={{0,4},{4,8},{8,12},{12,16},{16,20},{20,24},{24,28},{28,32},{32,36}... | collective-permute-start | bytes 3145736 | tf_op jit(solution)/shard_map/while/body/eval_jaxpr/ppermute | solution.py:12
  931.9 22.8 %collective-permute-start = (f32[512,512]{1,0:T(8,128)}, f32[512,512]{1,0:T(8,128)}, u32[]{:S(2)}, u32[]{:S(2)}) collective-permute-start(f32[512,512]{1,0:T(8,128)} %get-tuple-element.404), channel_id=1, source_target_pairs={{0,4},{4,8},{8,12},{12,16},{16,20},{20,24},{24,28},{28,32},{32,36}... | collective-permute-start | bytes 3145736 | tf_op jit(solution)/shard_map/while/body/eval_jaxpr/ppermute | solution.py:12
  975.6 22.7 %collective-permute-start = (f32[512,512]{1,0:T(8,128)}, f32[512,512]{1,0:T(8,128)}, u32[]{:S(2)}, u32[]{:S(2)}) collective-permute-start(f32[512,512]{1,0:T(8,128)} %get-tuple-element.404), channel_id=1, source_target_pairs={{0,4},{4,8},{8,12},{12,16},{16,20},{20,24},{24,28},{28,32},{32,36}... | collective-permute-start | bytes 3145736 | tf_op jit(solution)/shard_map/while/body/eval_jaxpr/ppermute | solution.py:12
  1019.2 22.5 %collective-permute-start = (f32[512,512]{1,0:T(8,128)}, f32[512,512]{1,0:T(8,128)}, u32[]{:S(2)}, u32[]{:S(2)}) collective-permute-start(f32[512,512]{1,0:T(8,128)} %get-tuple-element.404), channel_id=1, source_target_pairs={{0,4},{4,8},{8,12},{12,16},{16,20},{20,24},{24,28},{28,32},{32,36}... | collective-permute-start | bytes 3145736 | tf_op jit(solution)/shard_map/while/body/eval_jaxpr/ppermute | solution.py:12
  1105.8 22.2 %collective-permute-start = (f32[512,512]{1,0:T(8,128)}, f32[512,512]{1,0:T(8,128)}, u32[]{:S(2)}, u32[]{:S(2)}) collective-permute-start(f32[512,512]{1,0:T(8,128)} %get-tuple-element.404), channel_id=1, source_target_pairs={{0,4},{4,8},{8,12},{12,16},{16,20},{20,24},{24,28},{28,32},{32,36}... | collective-permute-start | bytes 3145736 | tf_op jit(solution)/shard_map/while/body/eval_jaxpr/ppermute | solution.py:12
  1192.0 22.2 %collective-permute-start = (f32[512,512]{1,0:T(8,128)}, f32[512,512]{1,0:T(8,128)}, u32[]{:S(2)}, u32[]{:S(2)}) collective-permute-start(f32[512,512]{1,0:T(8,128)} %get-tuple-element.404), channel_id=1, source_target_pairs={{0,4},{4,8},{8,12},{12,16},{16,20},{20,24},{24,28},{28,32},{32,36}... | collective-permute-start | bytes 3145736 | tf_op jit(solution)/shard_map/while/body/eval_jaxpr/ppermute | solution.py:12
  1278.3 22.2 %collective-permute-start = (f32[512,512]{1,0:T(8,128)}, f32[512,512]{1,0:T(8,128)}, u32[]{:S(2)}, u32[]{:S(2)}) collective-permute-start(f32[512,512]{1,0:T(8,128)} %get-tuple-element.404), channel_id=1, source_target_pairs={{0,4},{4,8},{8,12},{12,16},{16,20},{20,24},{24,28},{28,32},{32,36}... | collective-permute-start | bytes 3145736 | tf_op jit(solution)/shard_map/while/body/eval_jaxpr/ppermute | solution.py:12
  1321.4 22.2 %collective-permute-start = (f32[512,512]{1,0:T(8,128)}, f32[512,512]{1,0:T(8,128)}, u32[]{:S(2)}, u32[]{:S(2)}) collective-permute-start(f32[512,512]{1,0:T(8,128)} %get-tuple-element.404), channel_id=1, source_target_pairs={{0,4},{4,8},{8,12},{12,16},{16,20},{20,24},{24,28},{28,32},{32,36}... | collective-permute-start | bytes 3145736 | tf_op jit(solution)/shard_map/while/body/eval_jaxpr/ppermute | solution.py:12
  1407.6 22.2 %collective-permute-start = (f32[512,512]{1,0:T(8,128)}, f32[512,512]{1,0:T(8,128)}, u32[]{:S(2)}, u32[]{:S(2)}) collective-permute-start(f32[512,512]{1,0:T(8,128)} %get-tuple-element.404), channel_id=1, source_target_pairs={{0,4},{4,8},{8,12},{12,16},{16,20},{20,24},{24,28},{28,32},{32,36}... | collective-permute-start | bytes 3145736 | tf_op jit(solution)/shard_map/while/body/eval_jaxpr/ppermute | solution.py:12
  (79 other events, 2789.0 us)
Sparse Core Ops, SparseCore 0:
  1496.2 356.0 all-reduce.2
where the time goes:
time: 1970 us; the launch traced here: 1960 us
  waiting for transfers between devices  553 us (28%)
  other arithmetic  467 us (24%)
  starting transfers between devices  465 us (24%)
  matrix products  264 us (13%)
  local copies, waits for them, and re-layouts  164 us (8%)
  blocking collectives  28.3 us (1%)
    ppermute x66, starting transfers between devices, from_behind(): lax.ppermute(value, axis, [(source, source + steps) for source in range(f...  465 us
    psum x1, waiting for transfers between devices, from_root(): return lax.psum(block, axis)  356 us
    dot_general x165, matrix products, product(): jnp.dot(left, right, precision=lax.Precision.HIGHEST, preferred_element_t...  241 us
    another operation x99, other arithmetic, woodbury(): factor = jnp.linalg.cholesky(system)  240 us
    ppermute x66, waiting for transfers between devices, from_behind(): lax.ppermute(value, axis, [(source, source + steps) for source in range(f...  198 us
    another operation x66, other arithmetic, woodbury(): gain_rows = jax.scipy.linalg.cho_solve((factor, True), cross_term.T)  183 us
    psum x2, local copies, waits for them, and re-layouts, from_root(): return lax.psum(block, axis)  61.3 us
    dynamic_slice x33, local copies, waits for them, and re-layouts, one_turn(): old_est = lax.dynamic_index_in_dim(kept_est, clipped, 0, keepdims=False)  48.5 us
  transfers between devices with their start and end apart: 67, of which 34 were waited for; matrix products, arithmetic and copies ran while one was open for 7% of the time, Pallas kernels for 0%

commit v1 on v0

v1 whole, which is shorter than its diff:
```python
import functools

import jax
import jax.numpy as jnp
from jax import lax
from jax.experimental import pallas as pl
from jax.experimental.pallas import tpu as pltpu
from jax.sharding import PartitionSpec as P

prior_var = 0.1
TILE = 128
F32, BF16 = jnp.float32, jnp.bfloat16


def mm(left, right, dims=((1,), (0,))):
    return lax.dot_general(left, right, (dims, ((), ())), preferred_element_type=F32)


def exact(left, right):
    return jnp.dot(left, right, precision=lax.Precision.HIGHEST, preferred_element_type=F32)


def split(value):
    high = value.astype(BF16)
    return high, (value - high.astype(F32)).astype(BF16)


def prepare(pick_ref, channel_ref, received_ref, noise_ref, keep_ref, give_ref):
    mine = pick_ref[0]
    users = channel_ref.shape[-1]
    for which, out_ref in ((mine, keep_ref), (1 - mine, give_ref)):
        scale = 1.0 / jnp.sqrt(jnp.full((1, 1), noise_ref[which, 0], F32))
        out_ref[:, :users] = channel_ref[which] * scale
        out_ref[:, users:] = jnp.zeros(out_ref[:, users:].shape, F32)
        samples = received_ref[which].T
        out_ref[:, users : users + samples.shape[1]] = samples * scale


def gram(keep_ref, take_ref, out_ref):
    users, symbols = keep_ref.shape[1] - TILE, 32
    both = jnp.concatenate([keep_ref[...], take_ref[...]], axis=0)
    high, low = split(both)
    left = jnp.concatenate([high, high, low], axis=0).T
    right = jnp.concatenate([high, low, high], axis=0)
    tiles, at = users // TILE, 0
    for i in range(tiles):
        row = mm(left[i * TILE : (i + 1) * TILE], right[:, : (i + 1) * TILE])
        for j in range(i + 1):
            out_ref[at : at + TILE] = row[:, j * TILE : (j + 1) * TILE]
            at += TILE
    row = mm(left[users : users + symbols], right[:, :users])
    for j in range(tiles):
        out_ref[at : at + symbols] = row[:, j * TILE : (j + 1) * TILE]
        at += symbols


def eye_of(n):
    return lax.broadcasted_iota(jnp.int32, (n, n), 0) == lax.broadcasted_iota(jnp.int32, (n, n), 1)


def step_count(error):
    def more(state):
        return (state[1] > 0.0125) & (state[0] < 40)

    def step(state):
        square = state[1] * state[1]
        return state[0] + 1, square / (2.0 - square)

    return lax.while_loop(more, step, (jnp.int32(0), error))[0]


def invert(gram_ref, downlink_ref, rows_ref, diag_ref, a_ref, x_ref, e_ref, v_ref):
    n, symbols = a_ref.shape[0], downlink_ref.shape[0]
    tiles, at = n // TILE, 0
    prior = 1.0 / prior_var
    for i in range(tiles):
        for j in range(i + 1):
            tile = gram_ref[at : at + TILE]
            at += TILE
            if i == j:
                tile = tile + jnp.where(eye_of(TILE), prior, 0.0)
            else:
                a_ref[j * TILE : (j + 1) * TILE, i * TILE : (i + 1) * TILE] = tile.T
            a_ref[i * TILE : (i + 1) * TILE, j * TILE : (j + 1) * TILE] = tile
    mixed = jnp.concatenate([gram_ref[at + symbols * j : at + symbols * (j + 1)] for j in range(tiles)], axis=1)
    rows = jnp.concatenate([downlink_ref[...], mixed], axis=0)
    a = a_ref[...]
    eye = jnp.where(eye_of(n), 1.0, 0.0)
    top = jnp.max(jnp.sum(jnp.abs(a), axis=1)) * 1.0001
    alpha = 2.0 / (prior + top)
    start = (top - prior) / (top + prior)
    square = start * start
    gain, bound = 2.0 / (2.0 - square), square / (2.0 - square)
    first = (2.0 * alpha * gain) * eye - (alpha * alpha * gain) * a
    count = step_count(bound)
    a_high, a_low = split(a)
    x_ref[...] = first.astype(BF16)

    def step(index, bound):
        x = x_ref[...]
        left = (eye - mm(a_high, x)).astype(BF16)
        square = bound * bound
        gain = 2.0 / (2.0 - square)
        x_ref[...] = ((x.astype(F32) + mm(x, left)) * gain).astype(BF16)
        return square / (2.0 - square)

    lax.fori_loop(0, jnp.minimum(count, 6), step, bound)
    x = x_ref[...]
    error = eye - (mm(a_high, x) + mm(a_low, x))
    e = error.astype(BF16)
    twice = mm(e, e)
    e_ref[...] = error
    v_ref[...] = twice
    good = jnp.sum(twice * twice) < 1e-5

    @pl.when(good)
    def _():
        error = e_ref[...]
        twice = v_ref[...]
        e = error.astype(BF16)
        x = x_ref[...]
        update = mm(x, e)
        diag = jnp.where(eye_of(n), x.astype(F32) + update, 0.0) + (error + twice) * update
        diag_ref[...] = jnp.broadcast_to(jnp.sum(diag, axis=0)[None, None], diag_ref.shape)
        high, low = split(rows)
        z = mm(jnp.concatenate([high, low], axis=0), x)
        z = z[: 2 * symbols] + z[2 * symbols :]
        z = z + mm(z.astype(BF16), e)
        rows_ref[...] = z + mm(z.astype(BF16), twice.astype(BF16))

    @pl.when(jnp.logical_not(good))
    def _():
        e_ref[...] = first

        def step(index, bound):
            x = e_ref[...]
            square = bound * bound
            gain = 2.0 / (2.0 - square)
            e_ref[...] = (x + exact(x, eye - exact(a_ref[...], x))) * gain
            return square / (2.0 - square)

        lax.fori_loop(0, count + 2, step, bound)
        x = e_ref[...]
        diag = jnp.sum(jnp.where(eye_of(n), x, 0.0), axis=0)
        diag_ref[...] = jnp.broadcast_to(diag[None, None], diag_ref.shape)
        rows_ref[...] = exact(rows, x)


def finish(pick_ref, own_ref, other_ref, diag_ref, channel_ref, order_ref, transmit_ref, owned_ref):
    mine = pick_ref[0]
    blocks, symbols = transmit_ref.shape[0], transmit_ref.shape[1]
    mean_error = jnp.sum(diag_ref[...], axis=0) / diag_ref.shape[0]
    scale = lax.rsqrt(mean_error)
    scale = scale * (1.5 - 0.5 * mean_error * scale * scale)
    n = own_ref.shape[1]
    order = order_ref[...]
    pick = (lax.broadcasted_iota(jnp.int32, (n, order.shape[1]), 0) == order).astype(BF16)
    for block in range(blocks):
        z = jnp.where(mine == block, own_ref[...], other_ref[...])
        high, low = split(z[:symbols] * scale)
        h_high, h_low = split(channel_ref[block])
        left = jnp.concatenate([high, low], axis=0)
        one = mm(left, h_high, ((1,), (1,)))
        two = mm(high, h_low, ((1,), (1,)))
        transmit_ref[block] = one[:symbols] + (one[symbols:] + two)
        x = z[symbols:]
        high = x.astype(BF16)
        rest = x - high.astype(F32)
        middle, low = split(rest)
        parts = mm(jnp.concatenate([high, middle, low], axis=0), pick)
        owned_ref[block] = parts[:symbols] + (parts[symbols : 2 * symbols] + parts[2 * symbols :])


VMEM = pl.BlockSpec(memory_space=pltpu.VMEM)
SMEM = pl.BlockSpec(memory_space=pltpu.SMEM)


def call(body, outs, in_specs, name, scratch=()):
    return pl.pallas_call(
        body,
        out_shape=outs,
        in_specs=in_specs,
        out_specs=jax.tree.map(lambda _: VMEM, outs),
        scratch_shapes=scratch,
        name=name,
        compiler_params=pltpu.CompilerParams(vmem_limit_bytes=48 << 20),
    )


def shards(channel, received, noise_var, downlink, user_order):
    blocks, _, antennas, n = channel.shape
    symbols = received.shape[1]
    channel = channel.reshape(blocks, antennas, n)
    links, subs = lax.axis_size("stripe"), lax.axis_size("sub")
    pair, ring = 4, links // 8
    position = lax.axis_index("stripe")
    mine = (position // pair) % 2
    pick = mine.reshape(1).astype(jnp.int32)
    planes = [[x * 8 + y * pair + z for x in range(ring) for z in range(pair)] for y in range(2)]
    columns = [
        [(x * 8 + y * pair + z) * subs + s for y in range(2) for s in range(subs)]
        for x in range(ring)
        for z in range(pair)
    ]
    swap = [(i, i ^ pair) for i in range(links)]

    def struct(*shape):
        return jax.ShapeDtypeStruct(shape, F32)

    keep, give = call(prepare, (struct(antennas, n + TILE),) * 2, [SMEM, VMEM, VMEM, SMEM], "prepare")(
        pick, channel, received, noise_var
    )
    take = lax.ppermute(give, "stripe", swap)
    tiles = n // TILE
    height = tiles * (tiles + 1) // 2 * TILE + tiles * symbols
    group = len(planes[0])
    part = call(gram, struct(height, TILE), [VMEM, VMEM], "gram")(keep, take)
    part = part.reshape(group, height // group, TILE)
    part = lax.all_to_all(part, "stripe", 0, 0, axis_index_groups=planes, tiled=True)
    part = jnp.broadcast_to(jnp.sum(part, axis=0), part.shape)
    whole = lax.all_to_all(part, "stripe", 0, 0, axis_index_groups=planes, tiled=True)
    whole = whole.reshape(height, TILE)
    down = lax.dynamic_index_in_dim(downlink, mine, 0, keepdims=False)
    column = len(columns[0])
    rows, diag = call(
        invert,
        (struct(2 * symbols, n), struct(column, 1, n)),
        [VMEM, VMEM],
        "invert",
        [pltpu.VMEM((n, n), F32), pltpu.VMEM((n, n), BF16), pltpu.VMEM((n, n), F32), pltpu.VMEM((n, n), F32)],
    )(whole, down)
    other = lax.ppermute(rows, "stripe", swap)
    diags = lax.all_to_all(diag, ("stripe", "sub"), 0, 0, axis_index_groups=columns, tiled=True)
    return call(
        finish,
        (struct(blocks, symbols, antennas), struct(blocks, symbols, user_order.shape[0])),
        [SMEM, VMEM, VMEM, VMEM, VMEM, VMEM],
        "finish",
    )(pick, rows, other, diags, channel, user_order.reshape(1, -1))


def solution(mesh):
    return jax.shard_map(
        shards,
        mesh=mesh,
        in_specs=(
            P("sub", "stripe", None, None),
            P("sub", None, "stripe"),
            P("sub", "stripe"),
            P("sub", None, None),
            P("stripe"),
        ),
        out_specs=(P("sub", None, "stripe"), P("sub", None, "stripe")),
        check_vma=False,
    )
```

time: 1970 us -> 65.5 us (0.03)
  waiting for transfers between devices: 553 us -> 14.2 us
  other arithmetic: 467 us -> 0.04 us
  starting transfers between devices: 465 us -> 7.41 us
  matrix products: 264 us -> 0 us
  local copies, waits for them, and re-layouts: 164 us -> 3.99 us
    ppermute x66 -> x2, starting transfers between devices: 465 us -> 3.57 us  [the longest x1 2.19 us: shards(): take = lax.ppermute(give, 'stripe', swap)]
    another operation x165 -> x0, other arithmetic: 423 us -> none  [the longest x99 240 us: woodbury(): factor = jnp.linalg.cholesky(system)]
    psum x1 -> x0, waiting for transfers between devices: 356 us -> none  [from_root(): return lax.psum(block, axis)]
    dot_general x167 -> x0, matrix products: 245 us -> none  [the longest x165 241 us: product(): jnp.dot(left, right, precision=lax.Precision.HIGHEST, preferred_element_t...]
    ppermute x66 -> x2, waiting for transfers between devices: 198 us -> 3.57 us  [the longest x1 3.57 us: shards(): take = lax.ppermute(give, 'stripe', swap)]
    dynamic_slice x99 -> x0, local copies, waits for them, and re-layouts: 91.5 us -> none  [the longest x33 48.5 us: one_turn(): old_est = lax.dynamic_index_in_dim(kept_est, clipped, 0, keepdims=False)]
    psum x2 -> x0, local copies, waits for them, and re-layouts: 61.3 us -> none  [from_root(): return lax.psum(block, axis)]
    div x33 -> x0, other arithmetic: 39.6 us -> none  [woodbury(): factor = jnp.linalg.cholesky(system)]
  transfers between devices with their start and end apart: 67 -> 3, of which waited for: 34 -> 2; matrix products, arithmetic and copies ran while one was open for 7% -> 0% of each run, Pallas kernels for 0% -> 0%
where the time goes in v1:
time: 65.5 us; the launch traced here: 64.8 us
  blocking collectives  31.7 us (48%)
  waiting for transfers between devices  14.2 us (22%)
  starting transfers between devices  7.41 us (11%)
  Pallas kernels  6.69 us (10%)
  local copies, waits for them, and re-layouts  3.99 us (6%)
  between operations  0.74 us (1%)
    all_to_all x1, blocking collectives, shards(): lax.all_to_all(part, 'stripe', 0, 0, axis_index_groups=planes, tiled=True)  19 us
    all_to_all x1, blocking collectives, shards(): lax.all_to_all(diag, ('stripe', 'sub'), 0, 0, axis_index_groups=columns,...  12.7 us
    all_to_all x1, waiting for transfers between devices, shards(): lax.all_to_all(part, 'stripe', 0, 0, axis_index_groups=planes, tiled=True)  10.6 us
    pallas_call x1, Pallas kernels, shards(): call(invert, (struct(2 * symbols, n), struct(column, 1, n)), [VMEM, VMEM]...  4.76 us
    all_to_all x1, starting transfers between devices, shards(): lax.all_to_all(part, 'stripe', 0, 0, axis_index_groups=planes, tiled=True)  3.84 us
    ppermute x1, waiting for transfers between devices, shards(): take = lax.ppermute(give, 'stripe', swap)  3.57 us
    unnamed x13, local copies, waits for them, and re-layouts  2.39 us
    ppermute x1, starting transfers between devices, shards(): take = lax.ppermute(give, 'stripe', swap)  2.19 us
  transfers between devices with their start and end apart: 3, of which 2 were waited for; matrix products, arithmetic and copies ran while one was open for 0% of the time, Pallas kernels for 0%

profile of v1, /device:TPU:1, one launch (start us, length us, event | category | flops | bytes accessed | tf_op | source)
XLA Modules:
  0.0 64.8 jit_solution(2657871397399190320)
XLA Ops:
  0.6 0.0 copy-start
  0.6 0.0 copy-start.3
  0.7 0.0 copy-start.5
  0.7 0.7 %copy-done.5 = f32[2,1]{0,1:T(1,128)S(1)} copy-done((f32[2,1]{0,1:T(1,128)S(1)}, f32[2,1]{0,1:T(1,128)}, u32[]{:S(2)}) %copy-start.5) | copy-done | bytes 32
  1.4 0.1 copy.7.noise_ref
  1.5 0.0 copy-done.3
  1.5 0.9 %copy-done.1 = f32[2,1,64,512]{3,2,1,0:T(8,128)S(1)} copy-done((f32[2,1,64,512]{3,2,1,0:T(8,128)S(1)}, f32[2,1,64,512]{3,2,1,0:T(8,128)}, u32[]{:S(2)}) %copy-start.1) | copy-done | bytes 262168
  2.4 0.6 prepare.1
  3.1 2.2 %collective-permute-start = (f32[64,640]{1,0:T(8,128)S(1)}, f32[64,640]{1,0:T(8,128)S(1)}, u32[]{:S(2)}, u32[]{:S(2)}) collective-permute-start(f32[64,640]{1,0:T(8,128)S(1)} %get-tuple-element.7), channel_id=1, source_target_pairs={{0,16},{4,20},{8,24},{12,28},{16,0},{20,4},{24,8},{28,12},{32,48},... | collective-permute-start | bytes 491528 | tf_op jit(solution)/shard_map/ppermute | solution.py:213
  5.2 3.6 %collective-permute-done.take_ref = f32[64,640]{1,0:T(8,128)S(1)} collective-permute-done((f32[64,640]{1,0:T(8,128)S(1)}, f32[64,640]{1,0:T(8,128)S(1)}, u32[]{:S(2)}, u32[]{:S(2)}) %collective-permute-start) | collective-permute-done | bytes 163872 | tf_op jit(solution)/shard_map/ppermute | solution.py:213
  8.8 0.4 gram.1
  9.2 19.0 %all_to_all.15 = f32[16,88,128]{2,1,0:T(8,128)S(1)} all-to-all(f32[16,88,128]{2,1,0:T(8,128)S(1)} %bitcast.8), channel_id=1, replica_groups={{0,4,8,12,32,36,40,44,64,68,72,76,96,100,104,108},{16,20,24,28,48,52,56..., dimensions={0} | all-to-all | bytes 1441792 | tf_op jit(solution)/shard_map/all_to_all | solution.py:219
  28.3 0.9 %broadcast_in_dim.3 = f32[16,88,128]{2,1,0:T(8,128)} broadcast(f32[88,128]{1,0:T(8,128)S(1)} %reduce_sum.9), dimensions={1,2} | broadcast | bytes 765952 | tf_op jit(solution)/shard_map/broadcast_in_dim | solution.py:220
  29.2 3.8 %all-to-all-start.1 = ((f32[16,88,128]{2,1,0:T(8,128)}), f32[16,88,128]{2,1,0:T(8,128)S(1)}, u32[]{:S(2)}, u32[]{:S(2)}) async-start(f32[16,88,128]{2,1,0:T(8,128)} %broadcast_in_dim.3), calls=%async_computation.1 | async-start | bytes 1441792 | tf_op jit(solution)/shard_map/all_to_all | solution.py:221
  33.1 0.0 copy-done
  33.1 10.6 %all-to-all-done.1 = f32[16,88,128]{2,1,0:T(8,128)S(1)} async-done(((f32[16,88,128]{2,1,0:T(8,128)}), f32[16,88,128]{2,1,0:T(8,128)S(1)}, u32[]{:S(2)}, u32[]{:S(2)}) %all-to-all-start.1) | async-done | bytes 720928 | tf_op jit(solution)/shard_map/all_to_all | solution.py:221
  43.7 4.8 %invert.1 = (f32[64,512]{1,0:T(8,128)S(1)}, f32[8,1,512]{2,1,0:T(1,128)S(1)}) custom-call(f32[1408,128]{1,0:T(8,128)S(1)} %bitcast.7, f32[32,512]{1,0:T(8,128)S(1)} %dynamic-slice_bitcast_fusion.downlink_ref), custom_call_target="tpu_custom_call" | custom-call | tf_op jit(solution)/shard_map/invert/pallas_call | solution.py:225
  48.5 1.4 %collective-permute-start.1 = (f32[64,512]{1,0:T(8,128)S(1)}, f32[64,512]{1,0:T(8,128)S(1)}, u32[]{:S(2)}, u32[]{:S(2)}) collective-permute-start(f32[64,512]{1,0:T(8,128)S(1)} %get-tuple-element.8.own_ref), channel_id=1, source_target_pairs={{0,16},{4,20},{8,24},{12,28},{16,0},{20,4},{24,8},{28,12},{32,48},... | collective-permute-start | bytes 393224 | tf_op jit(solution)/shard_map/ppermute | solution.py:232
  49.9 12.7 %all_to_all.16.diag_ref = f32[8,1,512]{2,1,0:T(1,128)S(1)} all-to-all(f32[8,1,512]{2,1,0:T(1,128)S(1)} %get-tuple-element.9), channel_id=1, replica_groups={{0,1,2,3,16,17,18,19},{4,5,6,7,20,21,22,23},{8,9,10,11,24,25,26,27},{12..., dimensions={0} | all-to-all | bytes 32768 | tf_op jit(solution)/shard_map/all_to_all | solution.py:233
  62.6 0.0 collective-permute-done.1.other_ref
  62.6 0.0 copy-done.2
  62.6 0.6 copy-done.4
  63.3 0.9 %finish.1 = (f32[2,32,64]{2,1,0:T(8,128)}, f32[2,32,16]{2,1,0:T(8,128)S(1)}) custom-call(s32[1]{0:T(128)} %bitcast.pick_ref, f32[64,512]{1,0:T(8,128)S(1)} %get-tuple-element.8.own_ref, f32[64,512]{1,0:T(8,128)S(1)} %collective-permute-done.1.other_ref, f32[8,1,512]{2,1,0:T(1,128)S(1)} %all_to_all.16.diag_ref, f32[2,64,512]{2,1,0:T(8,128)S(1)} %bitcast.10, ...), custom_call_target="tpu_custom_call" | custom-call | tf_op jit(solution)/shard_map/finish/pallas_call | solution.py:234
  64.1 0.7 %copy.8 = f32[2,32,16]{1,2,0:T(8,128)} copy(f32[2,32,16]{2,1,0:T(8,128)S(1)} %get-tuple-element.11) | data formatting | bytes 8192 | tf_op jit(solution)/shard_map/finish/pallas_call | solution.py:234
  (5 shorter events, 0.1 us)
Async XLA Ops:
  0.6 32.4 %copy-start = (f32[2,32,512]{2,1,0:T(8,128)S(1)}, f32[2,32,512]{2,1,0:T(8,128)}, u32[]{:S(2)}) copy-start(f32[2,32,512]{2,1,0:T(8,128)} %param.8) | copy-start | bytes 393220
  0.6 0.8 %copy-start.3 = (f32[2,32,64]{2,1,0:T(8,128)S(1)}, f32[2,32,64]{2,1,0:T(8,128)}, u32[]{:S(2)}) copy-start(f32[2,32,64]{2,1,0:T(8,128)} %received_ref.1) | copy-start | bytes 49156
  0.7 0.7 %copy-start.5 = (f32[2,1]{0,1:T(1,128)S(1)}, f32[2,1]{0,1:T(1,128)}, u32[]{:S(2)}) copy-start(f32[2,1]{0,1:T(1,128)} %param.7) | copy-start | bytes 28
  1.5 1.0 %copy-start.1 = (f32[2,1,64,512]{3,2,1,0:T(8,128)S(1)}, f32[2,1,64,512]{3,2,1,0:T(8,128)}, u32[]{:S(2)}) copy-start(f32[2,1,64,512]{3,2,1,0:T(8,128)} %param.5) | copy-start | bytes 786436
  3.1 5.8 %collective-permute-start = (f32[64,640]{1,0:T(8,128)S(1)}, f32[64,640]{1,0:T(8,128)S(1)}, u32[]{:S(2)}, u32[]{:S(2)}) collective-permute-start(f32[64,640]{1,0:T(8,128)S(1)} %get-tuple-element.7), channel_id=1, source_target_pairs={{0,16},{4,20},{8,24},{12,28},{16,0},{20,4},{24,8},{28,12},{32,48},... | collective-permute-start | bytes 491528 | tf_op jit(solution)/shard_map/ppermute | solution.py:213
  29.2 14.5 %all-to-all-start.1 = ((f32[16,88,128]{2,1,0:T(8,128)}), f32[16,88,128]{2,1,0:T(8,128)S(1)}, u32[]{:S(2)}, u32[]{:S(2)}) async-start(f32[16,88,128]{2,1,0:T(8,128)} %broadcast_in_dim.3), calls=%async_computation.1 | async-start | bytes 1441792 | tf_op jit(solution)/shard_map/all_to_all | solution.py:221
  43.7 18.9 %copy-start.2 = (f32[2,1,64,512]{3,2,1,0:T(8,128)S(1)}, f32[2,1,64,512]{3,2,1,0:T(8,128)}, u32[]{:S(2)}) copy-start(f32[2,1,64,512]{3,2,1,0:T(8,128)} %param.5) | copy-start | bytes 786436
  48.5 14.1 %collective-permute-start.1 = (f32[64,512]{1,0:T(8,128)S(1)}, f32[64,512]{1,0:T(8,128)S(1)}, u32[]{:S(2)}, u32[]{:S(2)}) collective-permute-start(f32[64,512]{1,0:T(8,128)S(1)} %get-tuple-element.8.own_ref), channel_id=1, source_target_pairs={{0,16},{4,20},{8,24},{12,28},{16,0},{20,4},{24,8},{28,12},{32,48},... | collective-permute-start | bytes 393224 | tf_op jit(solution)/shard_map/ppermute | solution.py:232
  62.6 0.7 %copy-start.4 = (s32[16]{0:T(128)S(1)}, s32[16]{0:T(128)}, u32[]{:S(2)}) copy-start(s32[16]{0:T(128)} %param.9) | copy-start | bytes 196

commit v2 on v1

v2 whole, which is shorter than its diff:
```python
import functools

import jax
import jax.numpy as jnp
from jax import lax
from jax.experimental import pallas as pl
from jax.experimental.pallas import tpu as pltpu
from jax.sharding import PartitionSpec as P


prior_var = 0.1
TILE = 128
F32, BF16 = jnp.float32, jnp.bfloat16


def mm(left, right, dims=((1,), (0,))):
    return lax.dot_general(left, right, (dims, ((), ())), preferred_element_type=F32)


def exact(left, right):
    return jnp.dot(left, right, precision=lax.Precision.HIGHEST, preferred_element_type=F32)


def split(value):
    high = value.astype(BF16)
    return high, (value - high.astype(F32)).astype(BF16)


def enter(pick_ref, channel_ref, received_ref, noise_ref, order_ref, keep_ref, give_ref, kept_ref, samples, noise, sems):
    mine = pick_ref[0]
    antennas = channel_ref.shape[1]
    sides = ((mine, keep_ref), (1 - mine, give_ref))
    copies = [
        pltpu.make_async_copy(received_ref, samples, sems.at[0]),
        pltpu.make_async_copy(noise_ref, noise, sems.at[1]),
        pltpu.make_async_copy(order_ref, kept_ref, sems.at[2]),
    ] + [
        pltpu.make_async_copy(channel_ref.at[which], out_ref.at[pl.ds(0, antennas)], sems.at[3 + k])
        for k, (which, out_ref) in enumerate(sides)
    ]
    for copy in copies:
        copy.start()
    for copy in copies[:2]:
        copy.wait()
    for which, out_ref in sides:
        out_ref[antennas:] = jnp.full((8, out_ref.shape[1]), noise[which], F32)
        for k in range(samples.shape[1] // 8):
            out_ref[antennas:, k * TILE : k * TILE + antennas] = samples[which, 8 * k : 8 * k + 8]
    for copy in copies[2:]:
        copy.wait()


def gram(symbols, keep_ref, take_ref, out_ref):
    antennas, users = keep_ref.shape[0] - 8, keep_ref.shape[1]

    def scaled(ref):
        extra = ref[antennas:]
        scale = 1.0 / jnp.sqrt(extra[:1, antennas : antennas + 1])
        chunks = [extra[:, k * TILE : k * TILE + antennas] for k in range(symbols // 8)]
        return ref[:antennas] * scale, jnp.concatenate(chunks, axis=0) * scale

    own, own_samples = scaled(keep_ref)
    other, other_samples = scaled(take_ref)
    both = jnp.concatenate([own, other], axis=0)
    samples = jnp.concatenate([own_samples, other_samples], axis=1)
    high, low = split(both)
    left = jnp.concatenate([high, high, low], axis=0).T
    right = jnp.concatenate([high, low, high], axis=0)
    y_high, y_low = split(samples)
    mixed = mm(jnp.concatenate([y_high, y_high, y_low], axis=1), right)
    tiles, at = users // TILE, 0
    lower = lower_of(TILE)
    diagonal = []
    for i in range(tiles):
        row = mm(left[i * TILE : (i + 1) * TILE], right[:, : (i + 1) * TILE])
        for j in range(i):
            out_ref[at : at + TILE] = row[:, j * TILE : (j + 1) * TILE]
            at += TILE
        diagonal.append(row[:, i * TILE :])
    for i in range(0, tiles, 2):
        out_ref[at : at + TILE] = jnp.where(lower, diagonal[i], diagonal[i + 1])
        at += TILE
    for j in range(tiles):
        out_ref[at : at + symbols] = mixed[:, j * TILE : (j + 1) * TILE]
        at += symbols
    out_ref[at:] = jnp.zeros((out_ref.shape[0] - at, TILE), F32)
    for i in range(1, tiles, 2):
        out_ref[at : at + 1] = jnp.sum(jnp.where(eye_of(TILE), diagonal[i], 0.0), axis=0, keepdims=True)
        at += 1


def lower_of(n):
    return lax.broadcasted_iota(jnp.int32, (n, n), 0) >= lax.broadcasted_iota(jnp.int32, (n, n), 1)


def eye_of(n):
    return lax.broadcasted_iota(jnp.int32, (n, n), 0) == lax.broadcasted_iota(jnp.int32, (n, n), 1)


def step_count(error):
    def more(state):
        return (state[1] > 0.0125) & (state[0] < 40)

    def step(state):
        return state[0] + 1, after(state[1])

    return lax.while_loop(more, step, (jnp.int32(0), error))[0]


def after(bound):
    square = bound * bound
    return square / (2.0 - square)


def gain_of(bound):
    return 2.0 / (2.0 - bound * bound)


def invert(symbols, gram_ref, diag_ref, flag_ref, x_ref, e_ref, v_ref, a_ref, s_ref, t_ref):
    n = a_ref.shape[0]
    tiles, at = n // TILE, 0
    prior = 1.0 / prior_var
    lower, middle = lower_of(TILE), eye_of(TILE)
    tail = tiles * tiles // 2 * TILE + tiles * symbols

    def put(i, j, tile):
        a_ref[i * TILE : (i + 1) * TILE, j * TILE : (j + 1) * TILE] = tile

    for i in range(tiles):
        for j in range(i):
            tile = gram_ref[at : at + TILE]
            at += TILE
            put(i, j, tile)
            put(j, i, tile.T)
    for i in range(0, tiles, 2):
        tile = gram_ref[at : at + TILE]
        at += TILE
        flip = tile.T
        put(i, i, jnp.where(lower, tile, flip) + jnp.where(middle, prior, 0.0))
        row = gram_ref[tail + i // 2 : tail + i // 2 + 1] + prior
        put(i + 1, i + 1, jnp.where(middle, row, jnp.where(lower, flip, tile)))
    a = a_ref[...]
    eye = jnp.where(eye_of(n), 1.0, 0.0)
    top = jnp.max(jnp.sum(jnp.abs(a), axis=1)) * 1.0001
    alpha = 2.0 / (prior + top)
    start = (top - prior) / (top + prior)
    count = step_count(after(start))
    left = (eye - alpha * a).astype(BF16)
    s_ref[n:] = ((alpha * gain_of(start)) * (eye + left.astype(F32))).astype(BF16)

    def squared(product, bound):
        square = bound * bound
        return ((2.0 * product - square * eye) / (2.0 - square)).astype(BF16)

    s_ref[:n] = squared(mm(left, left), start)

    def step(index, bound):
        both = mm(s_ref[...], s_ref[:n])
        s_ref[n:] = (gain_of(bound) * (s_ref[n:].astype(F32) + both[n:])).astype(BF16)
        s_ref[:n] = squared(both[:n], bound)
        return after(bound)

    bound = lax.fori_loop(0, jnp.minimum(count, 7) - 1, step, after(start))
    x = s_ref[n:]
    x = (gain_of(bound) * (x.astype(F32) + mm(x, s_ref[:n]))).astype(BF16)
    x_ref[...] = x
    a_high, a_low = split(a)
    parts = mm(jnp.concatenate([a_high, a_low], axis=0), x)
    error = eye - (parts[:n] + parts[n:])
    e = error.astype(BF16)
    e_ref[...] = e
    both = mm(jnp.concatenate([e, x], axis=0), e)
    twice, update = both[:n], both[n:]
    v_ref[...] = twice.astype(BF16)
    diag = jnp.where(eye_of(n), x.astype(F32) + update, 0.0) + (error + twice) * update
    diag_ref[...] = jnp.sum(diag, axis=0, keepdims=True)
    good = jnp.sum(twice * twice) < 3e-5
    flag_ref[0] = good.astype(jnp.int32)

    @pl.when(jnp.logical_not(good))
    def _():
        a = a_ref[...]
        t_ref[...] = (alpha * gain_of(start)) * (2.0 * eye - alpha * a)

        def step(index, bound):
            x = t_ref[...]
            t_ref[...] = (x + exact(x, eye - exact(a_ref[...], x))) * gain_of(bound)
            return after(bound)

        lax.fori_loop(0, count + 2, step, after(start))
        x = t_ref[...]
        diag_ref[...] = jnp.sum(jnp.where(eye_of(n), x, 0.0), axis=0, keepdims=True)
        x_ref[...] = x.astype(BF16)
        e_ref[...], v_ref[...] = split(x - x.astype(BF16).astype(F32))


def apply(pick_ref, flag_ref, gram_ref, downlink_ref, x_ref, e_ref, v_ref, rows_ref):
    symbols, n = downlink_ref.shape[1:]
    tiles = n // TILE
    at = tiles * tiles // 2 * TILE
    mixed = jnp.concatenate([gram_ref[at + symbols * j : at + symbols * (j + 1)] for j in range(tiles)], axis=1)
    rows = jnp.concatenate([downlink_ref[pick_ref[0]], mixed], axis=0)
    good = flag_ref[0] == 1

    @pl.when(good)
    def _():
        high, low = split(rows)
        z = mm(jnp.concatenate([high, low], axis=0), x_ref[...])
        z = z[: 2 * symbols] + z[2 * symbols :]
        z = z + mm(z.astype(BF16), e_ref[...])
        rows_ref[...] = z + mm(z.astype(BF16), v_ref[...])

    @pl.when(jnp.logical_not(good))
    def _():
        x = x_ref[...].astype(F32) + (e_ref[...].astype(F32) + v_ref[...].astype(F32))
        rows_ref[...] = exact(rows, x)


def finish(terms, pick_ref, own_ref, other_ref, diag_ref, channel_ref, order_ref, transmit_ref, owned_ref):
    mine = pick_ref[0]
    blocks, symbols = transmit_ref.shape[0], transmit_ref.shape[1]
    mean_error = diag_ref[...] / terms
    scale = lax.rsqrt(mean_error)
    scale = scale * (1.5 - 0.5 * mean_error * scale * scale)
    n = own_ref.shape[1]
    order = order_ref[...]
    pick = (lax.broadcasted_iota(jnp.int32, (n, order.shape[1]), 0) == order).astype(BF16)
    for block in range(blocks):
        z = jnp.where(mine == block, own_ref[...], other_ref[...])
        high, low = split(z[:symbols] * scale)
        h_high, h_low = split(channel_ref[block])
        left = jnp.concatenate([high, low], axis=0)
        one = mm(left, h_high, ((1,), (1,)))
        two = mm(high, h_low, ((1,), (1,)))
        transmit_ref[block] = one[:symbols] + (one[symbols:] + two)
        x = z[symbols:]
        high = x.astype(BF16)
        rest = x - high.astype(F32)
        middle, low = split(rest)
        parts = mm(jnp.concatenate([high, middle, low], axis=0), pick)
        owned_ref[block] = (parts[:symbols] + (parts[symbols : 2 * symbols] + parts[2 * symbols :])).T


VMEM = pl.BlockSpec(memory_space=pltpu.VMEM)
SMEM = pl.BlockSpec(memory_space=pltpu.SMEM)


HBM = pl.BlockSpec(memory_space=pltpu.HBM)


def call(body, outs, in_specs, scratch=(), grant=48 << 20, outs_in=None, flops=None):
    return pl.pallas_call(
        body,
        out_shape=outs,
        in_specs=in_specs,
        out_specs=outs_in or jax.tree.map(lambda _: VMEM, outs),
        cost_estimate=flops and pl.CostEstimate(flops=flops, bytes_accessed=2 << 20, transcendentals=0),
        scratch_shapes=scratch,
        compiler_params=pltpu.CompilerParams(vmem_limit_bytes=grant),
    )


def shards(channel, received, noise_var, downlink, user_order):
    blocks, _, antennas, n = channel.shape
    symbols = received.shape[1]
    channel = channel.reshape(blocks, antennas, n)
    noise_var = noise_var.reshape(blocks)
    order = user_order.reshape(1, -1)
    links, subs = lax.axis_size("stripe"), lax.axis_size("sub")
    pair, ring = 4, links // 8
    mine = (lax.axis_index("stripe") // pair) % 2
    pick = mine.reshape(1).astype(jnp.int32)
    planes = [[x * 8 + y * pair + z for x in range(ring) for z in range(pair)] for y in range(2)]
    swap = [(i, i ^ pair) for i in range(links)]
    cores = [(i, i ^ 1) for i in range(subs)]
    across = [(i * subs + s, (i ^ pair) * subs + (s ^ 2)) for i in range(links) for s in range(subs)]

    def struct(*shape):
        return jax.ShapeDtypeStruct(shape, F32)

    def outside(value):
        return pltpu.with_memory_space_constraint(value, pltpu.HBM)

    keep, give, order = call(
        enter,
        (struct(antennas + 8, n), struct(antennas + 8, n), jax.ShapeDtypeStruct(order.shape, order.dtype)),
        [SMEM, HBM, HBM, HBM, HBM],
        [pltpu.VMEM(received.shape, F32), pltpu.SMEM((blocks,), F32), pltpu.SemaphoreType.DMA((5,))],
        8 << 20,
    )(pick, outside(channel), outside(received), outside(noise_var), outside(order))
    take = lax.ppermute(give, "stripe", swap)
    tiles, group = n // TILE, len(planes[0])
    used = tiles * tiles // 2 * TILE + tiles * symbols + tiles // 2
    height = -(-used // group) * group
    part = call(functools.partial(gram, symbols), struct(height, TILE), [VMEM, VMEM])(keep, take)
    part = part.reshape(height, 1, TILE)
    part = lax.all_to_all(part, "stripe", 0, 0, axis_index_groups=planes, tiled=True)
    part = lax.optimization_barrier(part.reshape(height, TILE))
    part = jnp.sum(part.reshape(group, height // group, TILE), axis=0)
    part = lax.optimization_barrier(jnp.broadcast_to(part, (group, *part.shape)).reshape(height, TILE))
    part = part.reshape(height, 1, TILE)
    whole = lax.all_to_all(part, "stripe", 0, 0, axis_index_groups=planes, tiled=True)
    whole = whole.reshape(height, TILE)
    half = jax.ShapeDtypeStruct((n, n), BF16)
    diag, flag, x, e, v = call(
        functools.partial(invert, symbols),
        (struct(1, n), jax.ShapeDtypeStruct((1,), jnp.int32), half, half, half),
        [VMEM],
        [pltpu.VMEM((n, n), F32), pltpu.VMEM((2 * n, n), BF16), pltpu.VMEM((n, n), F32)],
        outs_in=(VMEM, SMEM, VMEM, VMEM, VMEM),
    )(whole)
    rows = call(apply, struct(2 * symbols, n), [SMEM, SMEM] + [VMEM] * 5, flops=10**9)(
        pick, flag, whole, downlink, x, e, v
    )
    other = lax.ppermute(rows, "stripe", swap)
    diag = diag + lax.ppermute(diag, "sub", cores)
    diag = diag + lax.ppermute(diag, ("stripe", "sub"), across)
    diag = diag + lax.ppermute(diag, "stripe", swap)
    transmit, owned = call(
        functools.partial(finish, blocks * subs),
        (struct(blocks, symbols, antennas), struct(blocks, order.shape[1], symbols)),
        [SMEM, VMEM, VMEM, VMEM, VMEM, VMEM],
    )(pick, rows, other, diag, channel, order)
    return transmit, owned.transpose(0, 2, 1)


def solution(mesh):
    return jax.shard_map(
        shards,
        mesh=mesh,
        in_specs=(
            P("sub", "stripe", None, None),
            P("sub", None, "stripe"),
            P("sub", "stripe"),
            P("sub", None, None),
            P("stripe"),
        ),
        out_specs=(P("sub", None, "stripe"), P("sub", None, "stripe")),
        check_vma=False,
    )
```

time: 65.5 us -> 59.1 us (0.902)
  the two profiles are of different devices: /device:TPU:1 before, /device:TPU:0 now
where the time goes in v2:
time: 59.1 us; the launch traced here: 58.9 us
  blocking collectives  33 us (56%)
  waiting for transfers between devices  11.2 us (19%)
  Pallas kernels  8.14 us (14%)
  starting transfers between devices  5.6 us (9%)
  between operations  0.75 us (1%)
    all_to_all x2, blocking collectives, shards(): lax.all_to_all(part, 'stripe', 0, 0, axis_index_groups=planes, tiled=True)  33 us
    pallas_call x1, Pallas kernels, shards(): call(functools.partial(invert, symbols), (struct(1, n), jax.ShapeDtypeStr...  4.28 us
    ppermute x1, waiting for transfers between devices, shards(): take = lax.ppermute(give, 'stripe', swap)  3.85 us
    ppermute x1, waiting for transfers between devices, shards(): diag = diag + lax.ppermute(diag, 'stripe', swap)  3.58 us
    ppermute x1, waiting for transfers between devices, shards(): diag = diag + lax.ppermute(diag, ('stripe', 'sub'), across)  2.62 us
    ppermute x1, starting transfers between devices, shards(): diag = diag + lax.ppermute(diag, ('stripe', 'sub'), across)  2.17 us
    ppermute x1, starting transfers between devices, shards(): take = lax.ppermute(give, 'stripe', swap)  1.77 us
    ppermute x1, starting transfers between devices, shards(): other = lax.ppermute(rows, 'stripe', swap)  1.66 us
  transfers between devices with their start and end apart: 5, of which 4 were waited for; matrix products, arithmetic and copies ran while one was open for 0% of the time, Pallas kernels for 0%

profile of v2, /device:TPU:0, one launch (start us, length us, event | category | flops | bytes accessed | tf_op | source)
XLA Modules:
  0.0 58.9 jit_solution(7335621790659680669)
XLA Ops:
  0.7 1.0 %shard_map.68 = (f32[72,512]{1,0:T(8,128)S(1)}, f32[72,512]{1,0:T(8,128)S(1)}, s32[1,16]{1,0:T(1,128)S(1)}) custom-call(s32[1]{0:T(128)} %bitcast.pick_ref, f32[2,64,512]{2,1,0:T(8,128)} %bitcast.16, f32[2,32,64]{2,1,0:T(8,128)} %received_ref.1, f32[2]{0:T(128)} %bitcast.20, s32[1,16]{1,0:T(1,128)} %bitcast.21), custom_call_target="tpu_custom_call" | custom-call | tf_op jit(solution)/shard_map/pallas_call | solution.py:284
  1.7 1.8 %collective-permute-start = (f32[72,512]{1,0:T(8,128)S(1)}, f32[72,512]{1,0:T(8,128)S(1)}, u32[]{:S(2)}, u32[]{:S(2)}) collective-permute-start(f32[72,512]{1,0:T(8,128)S(1)} %get-tuple-element.13), channel_id=1, source_target_pairs={{0,16},{4,20},{8,24},{12,28},{16,0},{20,4},{24,8},{28,12},{32,48},... | collective-permute-start | bytes 442376 | tf_op jit(solution)/shard_map/ppermute | solution.py:291
  3.5 3.8 %collective-permute-done.take_ref = f32[72,512]{1,0:T(8,128)S(1)} collective-permute-done((f32[72,512]{1,0:T(8,128)S(1)}, f32[72,512]{1,0:T(8,128)S(1)}, u32[]{:S(2)}, u32[]{:S(2)}) %collective-permute-start) | collective-permute-done | bytes 147488 | tf_op jit(solution)/shard_map/ppermute | solution.py:291
  7.3 0.6 %shard_map.69 = f32[1168,128]{1,0:T(8,128)S(1)} custom-call(f32[72,512]{1,0:T(8,128)S(1)} %get-tuple-element.12.keep_ref, f32[72,512]{1,0:T(8,128)S(1)} %collective-permute-done.take_ref), custom_call_target="tpu_custom_call" | custom-call | tf_op jit(solution)/shard_map/pallas_call | solution.py:295
  7.9 19.3 %all_to_all.10 = f32[1168,1,128]{2,1,0:T(1,128)S(1)} all-to-all(f32[1168,1,128]{2,1,0:T(1,128)S(1)} %bitcast.15), channel_id=1, replica_groups={{0,4,8,12,32,36,40,44,64,68,72,76,96,100,104,108},{16,20,24,28,48,52,56..., dimensions={0} | all-to-all | bytes 1196032 | tf_op jit(solution)/shard_map/all_to_all | solution.py:297
  27.4 13.7 %all_to_all.11 = f32[1168,1,128]{2,1,0:T(1,128)S(1)} all-to-all(f32[1168,1,128]{2,1,0:T(1,128)S(1)} %bitcast.19), channel_id=1, replica_groups={{0,4,8,12,32,36,40,44,64,68,72,76,96,100,104,108},{16,20,24,28,48,52,56..., dimensions={0} | all-to-all | bytes 1196032 | tf_op jit(solution)/shard_map/all_to_all | solution.py:302
  41.1 0.0 copy-start.1
  41.1 4.3 %shard_map.70 = (f32[1,512]{1,0:T(1,128)S(1)}, s32[1]{0:T(128)}, bf16[512,512]{1,0:T(8,128)(2,1)S(1)}, bf16[512,512]{1,0:T(8,128)(2,1)S(1)}, bf16[512,512]{1,0:T(8,128)(2,1)S(1)}) custom-call(f32[1168,128]{1,0:T(8,128)S(1)} %bitcast.13), custom_call_target="tpu_custom_call" | custom-call | tf_op jit(solution)/shard_map/pallas_call | solution.py:305
  45.4 0.0 copy-done.1
  45.4 0.0 copy-start
  45.4 1.3 %shard_map.71.own_ref = f32[64,512]{1,0:T(8,128)S(1)} custom-call(s32[1]{0:T(128)} %bitcast.pick_ref, s32[1]{0:T(128)} %get-tuple-element.14.flag_ref, f32[1168,128]{1,0:T(8,128)S(1)} %bitcast.14, f32[2,32,512]{2,1,0:T(8,128)S(1)} %copy-done.1, bf16[512,512]{1,0:T(8,128)(2,1)S(1)} %get-tuple-element.15.x_ref, bf16[512,512]{1,0:T(8,128)(2,1)S(1)} %get-tuple-element.16.e_ref, ...), custom_call_target="tpu_custom_call" | custom-call | flops 1000000000 | bytes 2097152 | tf_op jit(solution)/shard_map/pallas_call | solution.py:312
  46.7 1.7 %collective-permute-start.1 = (f32[64,512]{1,0:T(8,128)S(1)}, f32[64,512]{1,0:T(8,128)S(1)}, u32[]{:S(2)}, u32[]{:S(2)}) collective-permute-start(f32[64,512]{1,0:T(8,128)S(1)} %shard_map.71.own_ref), channel_id=1, source_target_pairs={{0,16},{4,20},{8,24},{12,28},{16,0},{20,4},{24,8},{28,12},{32,48},... | collective-permute-start | bytes 393224 | tf_op jit(solution)/shard_map/ppermute | solution.py:315
  48.4 0.0 collective-permute-start.2
  48.4 1.2 %collective-permute-done.2 = f32[1,512]{1,0:T(1,128)S(1)} collective-permute-done((f32[1,512]{1,0:T(1,128)S(1)}, f32[1,512]{1,0:T(1,128)S(1)}, u32[]{:S(2)}, u32[]{:S(2)}) %collective-permute-start.2) | collective-permute-done | bytes 2080 | tf_op jit(solution)/shard_map/ppermute | solution.py:316
  49.5 2.2 %collective-permute-start.3 = (f32[1,512]{1,0:T(1,128)S(1)}, f32[1,512]{1,0:T(1,128)S(1)}, u32[]{:S(2)}, u32[]{:S(2)}) collective-permute-start(f32[1,512]{1,0:T(1,128)S(1)} %add.15), channel_id=1, source_target_pairs={{0,18},{1,19},{2,16},{3,17},{4,22},{5,23},{6,20},{7,21},{8,26},{9,... | collective-permute-start | bytes 6152 | tf_op jit(solution)/shard_map/ppermute | solution.py:317
  51.7 2.6 %collective-permute-done.3 = f32[1,512]{1,0:T(1,128)S(1)} collective-permute-done((f32[1,512]{1,0:T(1,128)S(1)}, f32[1,512]{1,0:T(1,128)S(1)}, u32[]{:S(2)}, u32[]{:S(2)}) %collective-permute-start.3) | collective-permute-done | bytes 2080 | tf_op jit(solution)/shard_map/ppermute | solution.py:317
  54.3 0.0 collective-permute-start.4
  54.3 3.6 %collective-permute-done.4 = f32[1,512]{1,0:T(1,128)S(1)} collective-permute-done((f32[1,512]{1,0:T(1,128)S(1)}, f32[1,512]{1,0:T(1,128)S(1)}, u32[]{:S(2)}, u32[]{:S(2)}) %collective-permute-start.4) | collective-permute-done | bytes 2080 | tf_op jit(solution)/shard_map/ppermute | solution.py:318
  57.9 0.0 collective-permute-done.1.other_ref
  57.9 0.0 copy-done
  57.9 1.0 %shard_map.72 = (f32[2,32,64]{2,1,0:T(8,128)}, f32[2,16,32]{2,1,0:T(8,128)}) custom-call(s32[1]{0:T(128)} %bitcast.pick_ref, f32[64,512]{1,0:T(8,128)S(1)} %shard_map.71.own_ref, f32[64,512]{1,0:T(8,128)S(1)} %collective-permute-done.1.other_ref, f32[1,512]{1,0:T(1,128)S(1)} %add.17.diag_ref, f32[2,64,512]{2,1,0:T(8,128)S(1)} %bitcast.17, ...), custom_call_target="tpu_custom_call" | custom-call | tf_op jit(solution)/shard_map/pallas_call | solution.py:319
  (7 shorter events, 0.2 us)
Async XLA Ops:
  1.7 5.6 %collective-permute-start = (f32[72,512]{1,0:T(8,128)S(1)}, f32[72,512]{1,0:T(8,128)S(1)}, u32[]{:S(2)}, u32[]{:S(2)}) collective-permute-start(f32[72,512]{1,0:T(8,128)S(1)} %get-tuple-element.13), channel_id=1, source_target_pairs={{0,16},{4,20},{8,24},{12,28},{16,0},{20,4},{24,8},{28,12},{32,48},... | collective-permute-start | bytes 442376 | tf_op jit(solution)/shard_map/ppermute | solution.py:291
  41.1 4.3 %copy-start.1 = (f32[2,32,512]{2,1,0:T(8,128)S(1)}, f32[2,32,512]{2,1,0:T(8,128)}, u32[]{:S(2)}) copy-start(f32[2,32,512]{2,1,0:T(8,128)} %downlink_ref.1) | copy-start | bytes 393220
  45.4 12.5 %copy-start = (f32[2,1,64,512]{3,2,1,0:T(8,128)S(1)}, f32[2,1,64,512]{3,2,1,0:T(8,128)}, u32[]{:S(2)}) copy-start(f32[2,1,64,512]{3,2,1,0:T(8,128)} %param.5) | copy-start | bytes 786436
  46.7 11.2 %collective-permute-start.1 = (f32[64,512]{1,0:T(8,128)S(1)}, f32[64,512]{1,0:T(8,128)S(1)}, u32[]{:S(2)}, u32[]{:S(2)}) collective-permute-start(f32[64,512]{1,0:T(8,128)S(1)} %shard_map.71.own_ref), channel_id=1, source_target_pairs={{0,16},{4,20},{8,24},{12,28},{16,0},{20,4},{24,8},{28,12},{32,48},... | collective-permute-start | bytes 393224 | tf_op jit(solution)/shard_map/ppermute | solution.py:315
  48.4 1.2 %collective-permute-start.2 = (f32[1,512]{1,0:T(1,128)S(1)}, f32[1,512]{1,0:T(1,128)S(1)}, u32[]{:S(2)}, u32[]{:S(2)}) collective-permute-start(f32[1,512]{1,0:T(1,128)S(1)} %get-tuple-element.18), channel_id=1, source_target_pairs={{0,1},{1,0},{2,3},{3,2},{4,5},{5,4},{6,7},{7,6},{8,9},{9,8},{10,11... | collective-permute-start | bytes 6152 | tf_op jit(solution)/shard_map/ppermute | solution.py:316
  49.5 4.8 %collective-permute-start.3 = (f32[1,512]{1,0:T(1,128)S(1)}, f32[1,512]{1,0:T(1,128)S(1)}, u32[]{:S(2)}, u32[]{:S(2)}) collective-permute-start(f32[1,512]{1,0:T(1,128)S(1)} %add.15), channel_id=1, source_target_pairs={{0,18},{1,19},{2,16},{3,17},{4,22},{5,23},{6,20},{7,21},{8,26},{9,... | collective-permute-start | bytes 6152 | tf_op jit(solution)/shard_map/ppermute | solution.py:317
  54.3 3.6 %collective-permute-start.4 = (f32[1,512]{1,0:T(1,128)S(1)}, f32[1,512]{1,0:T(1,128)S(1)}, u32[]{:S(2)}, u32[]{:S(2)}) collective-permute-start(f32[1,512]{1,0:T(1,128)S(1)} %add.16), channel_id=1, source_target_pairs={{0,16},{4,20},{8,24},{12,28},{16,0},{20,4},{24,8},{28,12},{32,48},... | collective-permute-start | bytes 6152 | tf_op jit(solution)/shard_map/ppermute | solution.py:318

commit v3 on v2

--- a/solution.py
+++ b/solution.py
@@ -26,8 +26,12 @@
     return high, (value - high.astype(F32)).astype(BF16)
 
 
-def enter(pick_ref, channel_ref, received_ref, noise_ref, order_ref, keep_ref, give_ref, kept_ref, samples, noise, sems):
-    mine = pick_ref[0]
+def kept_block():
+    return lax.bitwise_and(lax.shift_right_logical(lax.axis_index("stripe"), 2), 1)
+
+
+def enter(channel_ref, received_ref, noise_ref, order_ref, keep_ref, give_ref, kept_ref, samples, noise, sems):
+    mine = kept_block()
     antennas = channel_ref.shape[1]
     sides = ((mine, keep_ref), (1 - mine, give_ref))
     copies = [
@@ -97,16 +101,6 @@
     return lax.broadcasted_iota(jnp.int32, (n, n), 0) == lax.broadcasted_iota(jnp.int32, (n, n), 1)
 
 
-def step_count(error):
-    def more(state):
-        return (state[1] > 0.0125) & (state[0] < 40)
-
-    def step(state):
-        return state[0] + 1, after(state[1])
-
-    return lax.while_loop(more, step, (jnp.int32(0), error))[0]
-
-
 def after(bound):
     square = bound * bound
     return square / (2.0 - square)
@@ -116,7 +110,7 @@
     return 2.0 / (2.0 - bound * bound)
 
 
-def invert(symbols, gram_ref, diag_ref, flag_ref, x_ref, e_ref, v_ref, a_ref, s_ref, t_ref):
+def invert(symbols, gram_ref, diag_ref, flag_ref, x_ref, e_ref, v_ref, a_ref, s_ref, t_ref, u_ref, w_ref):
     n = a_ref.shape[0]
     tiles, at = n // TILE, 0
     prior = 1.0 / prior_var
@@ -141,18 +135,24 @@
         put(i + 1, i + 1, jnp.where(middle, row, jnp.where(lower, flip, tile)))
     a = a_ref[...]
     eye = jnp.where(eye_of(n), 1.0, 0.0)
-    top = jnp.max(jnp.sum(jnp.abs(a), axis=1)) * 1.0001
+    top = jnp.max(jnp.sum(jnp.abs(a), axis=0, keepdims=True), axis=1, keepdims=True) * 1.0001
     alpha = 2.0 / (prior + top)
     start = (top - prior) / (top + prior)
-    count = step_count(after(start))
     left = (eye - alpha * a).astype(BF16)
     s_ref[n:] = ((alpha * gain_of(start)) * (eye + left.astype(F32))).astype(BF16)
 
     def squared(product, bound):
         square = bound * bound
-        return ((2.0 * product - square * eye) / (2.0 - square)).astype(BF16)
+        scale = 1.0 / (2.0 - square)
+        return ((2.0 * scale) * product - (square * scale) * eye).astype(BF16)
 
     s_ref[:n] = squared(mm(left, left), start)
+    first = after(start)
+    bound, steps = first, jnp.zeros((1, 1), F32)
+    for _ in range(10):
+        bound = after(bound)
+        steps = steps + jnp.where(bound > 0.0125, 1.0, 0.0)
+    steps = jnp.max(steps).astype(jnp.int32)
 
     def step(index, bound):
         both = mm(s_ref[...], s_ref[:n])
@@ -160,11 +160,11 @@
         s_ref[:n] = squared(both[:n], bound)
         return after(bound)
 
-    bound = lax.fori_loop(0, jnp.minimum(count, 7) - 1, step, after(start))
+    bound = lax.fori_loop(0, steps, step, first)
     x = s_ref[n:]
     x = (gain_of(bound) * (x.astype(F32) + mm(x, s_ref[:n]))).astype(BF16)
     x_ref[...] = x
-    a_high, a_low = split(a)
+    a_high, a_low = split(a_ref[...])
     parts = mm(jnp.concatenate([a_high, a_low], axis=0), x)
     error = eye - (parts[:n] + parts[n:])
     e = error.astype(BF16)
@@ -179,27 +179,70 @@
 
     @pl.when(jnp.logical_not(good))
     def _():
-        a = a_ref[...]
-        t_ref[...] = (alpha * gain_of(start)) * (2.0 * eye - alpha * a)
-
-        def step(index, bound):
-            x = t_ref[...]
-            t_ref[...] = (x + exact(x, eye - exact(a_ref[...], x))) * gain_of(bound)
-            return after(bound)
-
-        lax.fori_loop(0, count + 2, step, after(start))
-        x = t_ref[...]
-        diag_ref[...] = jnp.sum(jnp.where(eye_of(n), x, 0.0), axis=0, keepdims=True)
-        x_ref[...] = x.astype(BF16)
-        e_ref[...], v_ref[...] = split(x - x.astype(BF16).astype(F32))
-
-
-def apply(pick_ref, flag_ref, gram_ref, downlink_ref, x_ref, e_ref, v_ref, rows_ref):
+        full(prior, top, start, a_ref, t_ref, u_ref, w_ref, diag_ref, x_ref, e_ref, v_ref)
+
+
+def full(prior, top, start, a_ref, t_ref, u_ref, w_ref, diag_ref, x_ref, e_ref, v_ref):
+    n = a_ref.shape[0]
+    tiles = n // TILE
+
+    def over(body):
+        def one(index, carry):
+            i, j = index // tiles, index % tiles
+            rows, columns = (pl.ds(pl.multiple_of(k * TILE, TILE), TILE) for k in (i, j))
+            body(rows, columns, jnp.where(eye_of(TILE) & (i == j), 1.0, 0.0))
+            return carry
+
+        lax.fori_loop(0, tiles * tiles, one, 0)
+
+    gain = (2.0 / (prior + top)) * gain_of(start)
+
+    def begin(rows, columns, eye):
+        t_ref[rows, columns] = gain * (2.0 * eye - (2.0 / (prior + top)) * a_ref[rows, columns])
+
+    over(begin)
+
+    first = after(start)
+
+    def more(index, carry):
+        bound = after(carry[0])
+        return bound, carry[1] + jnp.where(carry[0] > 1e-3, 1.0, 0.0)
+
+    steps = lax.fori_loop(0, 40, more, (first, jnp.zeros((1, 1), F32)))[1]
+
+    def step(index, bound):
+        def residual(rows, columns, eye):
+            u_ref[rows, columns] = eye - exact(a_ref[rows, :], t_ref[:, columns])
+
+        def update(rows, columns, eye):
+            w_ref[rows, columns] = gain_of(bound) * (t_ref[rows, columns] + exact(t_ref[rows, :], u_ref[:, columns]))
+
+        def back(rows, columns, eye):
+            t_ref[rows, columns] = w_ref[rows, columns]
+
+        over(residual)
+        over(update)
+        over(back)
+        return after(bound)
+
+    lax.fori_loop(0, jnp.max(steps).astype(jnp.int32) + 2, step, first)
+    diag_ref[...] = jnp.zeros(diag_ref.shape, F32)
+
+    def finish(rows, columns, eye):
+        x = t_ref[rows, columns]
+        diag_ref[:, columns] = diag_ref[:, columns] + jnp.sum(x * eye, axis=0, keepdims=True)
+        x_ref[rows, columns] = x.astype(BF16)
+        e_ref[rows, columns], v_ref[rows, columns] = split(x - x.astype(BF16).astype(F32))
+
+    over(finish)
+
+
+def apply(flag_ref, gram_ref, downlink_ref, x_ref, e_ref, v_ref, rows_ref):
     symbols, n = downlink_ref.shape[1:]
     tiles = n // TILE
     at = tiles * tiles // 2 * TILE
     mixed = jnp.concatenate([gram_ref[at + symbols * j : at + symbols * (j + 1)] for j in range(tiles)], axis=1)
-    rows = jnp.concatenate([downlink_ref[pick_ref[0]], mixed], axis=0)
+    rows = jnp.concatenate([downlink_ref[kept_block()], mixed], axis=0)
     good = flag_ref[0] == 1
 
     @pl.when(good)
@@ -216,8 +259,8 @@
         rows_ref[...] = exact(rows, x)
 
 
-def finish(terms, pick_ref, own_ref, other_ref, diag_ref, channel_ref, order_ref, transmit_ref, owned_ref):
-    mine = pick_ref[0]
+def finish(terms, own_ref, other_ref, diag_ref, channel_ref, order_ref, transmit_ref, owned_ref):
+    mine = kept_block()
     blocks, symbols = transmit_ref.shape[0], transmit_ref.shape[1]
     mean_error = diag_ref[...] / terms
     scale = lax.rsqrt(mean_error)
@@ -268,8 +311,6 @@
     order = user_order.reshape(1, -1)
     links, subs = lax.axis_size("stripe"), lax.axis_size("sub")
     pair, ring = 4, links // 8
-    mine = (lax.axis_index("stripe") // pair) % 2
-    pick = mine.reshape(1).astype(jnp.int32)
     planes = [[x * 8 + y * pair + z for x in range(ring) for z in range(pair)] for y in range(2)]
     swap = [(i, i ^ pair) for i in range(links)]
     cores = [(i, i ^ 1) for i in range(subs)]
@@ -284,10 +325,10 @@
     keep, give, order = call(
         enter,
         (struct(antennas + 8, n), struct(antennas + 8, n), jax.ShapeDtypeStruct(order.shape, order.dtype)),
-        [SMEM, HBM, HBM, HBM, HBM],
+        [HBM] * 4,
         [pltpu.VMEM(received.shape, F32), pltpu.SMEM((blocks,), F32), pltpu.SemaphoreType.DMA((5,))],
         8 << 20,
-    )(pick, outside(channel), outside(received), outside(noise_var), outside(order))
+    )(outside(channel), outside(received), outside(noise_var), outside(order))
     take = lax.ppermute(give, "stripe", swap)
     tiles, group = n // TILE, len(planes[0])
     used = tiles * tiles // 2 * TILE + tiles * symbols + tiles // 2
@@ -306,12 +347,10 @@
         functools.partial(invert, symbols),
         (struct(1, n), jax.ShapeDtypeStruct((1,), jnp.int32), half, half, half),
         [VMEM],
-        [pltpu.VMEM((n, n), F32), pltpu.VMEM((2 * n, n), BF16), pltpu.VMEM((n, n), F32)],
+        [pltpu.VMEM((n, n), F32), pltpu.VMEM((2 * n, n), BF16)] + [pltpu.VMEM((n, n), F32)] * 3,
         outs_in=(VMEM, SMEM, VMEM, VMEM, VMEM),
     )(whole)
-    rows = call(apply, struct(2 * symbols, n), [SMEM, SMEM] + [VMEM] * 5, flops=10**9)(
-        pick, flag, whole, downlink, x, e, v
-    )
+    rows = call(apply, struct(2 * symbols, n), [SMEM] + [VMEM] * 5, flops=10**9)(flag, whole, downlink, x, e, v)
     other = lax.ppermute(rows, "stripe", swap)
     diag = diag + lax.ppermute(diag, "sub", cores)
     diag = diag + lax.ppermute(diag, ("stripe", "sub"), across)
@@ -319,8 +358,8 @@
     transmit, owned = call(
         functools.partial(finish, blocks * subs),
         (struct(blocks, symbols, antennas), struct(blocks, order.shape[1], symbols)),
-        [SMEM, VMEM, VMEM, VMEM, VMEM, VMEM],
-    )(pick, rows, other, diag, channel, order)
+        [VMEM] * 5,
+    )(rows, other, diag, channel, order)
     return transmit, owned.transpose(0, 2, 1)
 
 

time: 59.1 us -> 58.8 us (level)
  no operation moved by 1% of the time
where the time goes in v3:
time: 58.8 us; the launch traced here: 58.6 us
  blocking collectives  33 us (56%)
  waiting for transfers between devices  11.2 us (19%)
  Pallas kernels  7.86 us (13%)
  starting transfers between devices  5.62 us (10%)
  between operations  0.72 us (1%)
    all_to_all x2, blocking collectives, shards(): lax.all_to_all(part, 'stripe', 0, 0, axis_index_groups=planes, tiled=True)  33 us
    pallas_call x1, Pallas kernels, shards(): call(functools.partial(invert, symbols), (struct(1, n), jax.ShapeDtypeStr...  4 us
    ppermute x1, waiting for transfers between devices, shards(): take = lax.ppermute(give, 'stripe', swap)  3.85 us
    ppermute x1, waiting for transfers between devices, shards(): diag = diag + lax.ppermute(diag, 'stripe', swap)  3.58 us
    ppermute x1, waiting for transfers between devices, shards(): diag = diag + lax.ppermute(diag, ('stripe', 'sub'), across)  2.61 us
    ppermute x1, starting transfers between devices, shards(): diag = diag + lax.ppermute(diag, ('stripe', 'sub'), across)  2.18 us
    ppermute x1, starting transfers between devices, shards(): take = lax.ppermute(give, 'stripe', swap)  1.77 us
    ppermute x1, starting transfers between devices, shards(): other = lax.ppermute(rows, 'stripe', swap)  1.67 us
  transfers between devices with their start and end apart: 5, of which 4 were waited for; matrix products, arithmetic and copies ran while one was open for 0% of the time, Pallas kernels for 0%

profile of v3, /device:TPU:0, one launch (start us, length us, event | category | flops | bytes accessed | tf_op | source)
XLA Modules:
  0.0 58.6 jit_solution(17327879366107074503)
XLA Ops:
  0.6 1.0 %shard_map.68 = (f32[72,512]{1,0:T(8,128)S(1)}, f32[72,512]{1,0:T(8,128)S(1)}, s32[1,16]{1,0:T(1,128)S(1)}) custom-call(f32[2,64,512]{2,1,0:T(8,128)} %bitcast.15, f32[2,32,64]{2,1,0:T(8,128)} %received_ref.1, f32[2]{0:T(128)} %bitcast.19, s32[1,16]{1,0:T(1,128)} %bitcast.20), custom_call_target="tpu_custom_call" | custom-call | tf_op jit(solution)/shard_map/pallas_call | solution.py:325
  1.7 1.8 %collective-permute-start = (f32[72,512]{1,0:T(8,128)S(1)}, f32[72,512]{1,0:T(8,128)S(1)}, u32[]{:S(2)}, u32[]{:S(2)}) collective-permute-start(f32[72,512]{1,0:T(8,128)S(1)} %get-tuple-element.13), channel_id=1, source_target_pairs={{0,16},{4,20},{8,24},{12,28},{16,0},{20,4},{24,8},{28,12},{32,48},... | collective-permute-start | bytes 442376 | tf_op jit(solution)/shard_map/ppermute | solution.py:332
  3.5 3.8 %collective-permute-done.take_ref = f32[72,512]{1,0:T(8,128)S(1)} collective-permute-done((f32[72,512]{1,0:T(8,128)S(1)}, f32[72,512]{1,0:T(8,128)S(1)}, u32[]{:S(2)}, u32[]{:S(2)}) %collective-permute-start) | collective-permute-done | bytes 147488 | tf_op jit(solution)/shard_map/ppermute | solution.py:332
  7.3 0.6 %shard_map.69 = f32[1168,128]{1,0:T(8,128)S(1)} custom-call(f32[72,512]{1,0:T(8,128)S(1)} %get-tuple-element.12.keep_ref, f32[72,512]{1,0:T(8,128)S(1)} %collective-permute-done.take_ref), custom_call_target="tpu_custom_call" | custom-call | tf_op jit(solution)/shard_map/pallas_call | solution.py:336
  7.9 19.3 %all_to_all.10 = f32[1168,1,128]{2,1,0:T(1,128)S(1)} all-to-all(f32[1168,1,128]{2,1,0:T(1,128)S(1)} %bitcast.14), channel_id=1, replica_groups={{0,4,8,12,32,36,40,44,64,68,72,76,96,100,104,108},{16,20,24,28,48,52,56..., dimensions={0} | all-to-all | bytes 1196032 | tf_op jit(solution)/shard_map/all_to_all | solution.py:338
  27.4 13.7 %all_to_all.11 = f32[1168,1,128]{2,1,0:T(1,128)S(1)} all-to-all(f32[1168,1,128]{2,1,0:T(1,128)S(1)} %bitcast.18), channel_id=1, replica_groups={{0,4,8,12,32,36,40,44,64,68,72,76,96,100,104,108},{16,20,24,28,48,52,56..., dimensions={0} | all-to-all | bytes 1196032 | tf_op jit(solution)/shard_map/all_to_all | solution.py:343
  41.1 0.0 copy-start.1
  41.1 4.0 %shard_map.70 = (f32[1,512]{1,0:T(1,128)S(1)}, s32[1]{0:T(128)}, bf16[512,512]{1,0:T(8,128)(2,1)S(1)}, bf16[512,512]{1,0:T(8,128)(2,1)S(1)}, bf16[512,512]{1,0:T(8,128)(2,1)S(1)}) custom-call(f32[1168,128]{1,0:T(8,128)S(1)} %bitcast.12), custom_call_target="tpu_custom_call" | custom-call | tf_op jit(solution)/shard_map/pallas_call | solution.py:346
  45.1 0.0 copy-done.1
  45.1 0.0 copy-start
  45.1 1.3 %shard_map.71.own_ref = f32[64,512]{1,0:T(8,128)S(1)} custom-call(s32[1]{0:T(128)} %get-tuple-element.14.flag_ref, f32[1168,128]{1,0:T(8,128)S(1)} %bitcast.13, f32[2,32,512]{2,1,0:T(8,128)S(1)} %copy-done.1, bf16[512,512]{1,0:T(8,128)(2,1)S(1)} %get-tuple-element.15.x_ref, bf16[512,512]{1,0:T(8,128)(2,1)S(1)} %get-tuple-element.16.e_ref, ...), custom_call_target="tpu_custom_call" | custom-call | flops 1000000000 | bytes 2097152 | tf_op jit(solution)/shard_map/pallas_call | solution.py:353
  46.4 1.7 %collective-permute-start.1 = (f32[64,512]{1,0:T(8,128)S(1)}, f32[64,512]{1,0:T(8,128)S(1)}, u32[]{:S(2)}, u32[]{:S(2)}) collective-permute-start(f32[64,512]{1,0:T(8,128)S(1)} %shard_map.71.own_ref), channel_id=1, source_target_pairs={{0,16},{4,20},{8,24},{12,28},{16,0},{20,4},{24,8},{28,12},{32,48},... | collective-permute-start | bytes 393224 | tf_op jit(solution)/shard_map/ppermute | solution.py:354
  48.1 0.0 collective-permute-start.2
  48.1 1.2 %collective-permute-done.2 = f32[1,512]{1,0:T(1,128)S(1)} collective-permute-done((f32[1,512]{1,0:T(1,128)S(1)}, f32[1,512]{1,0:T(1,128)S(1)}, u32[]{:S(2)}, u32[]{:S(2)}) %collective-permute-start.2) | collective-permute-done | bytes 2080 | tf_op jit(solution)/shard_map/ppermute | solution.py:355
  49.2 2.2 %collective-permute-start.3 = (f32[1,512]{1,0:T(1,128)S(1)}, f32[1,512]{1,0:T(1,128)S(1)}, u32[]{:S(2)}, u32[]{:S(2)}) collective-permute-start(f32[1,512]{1,0:T(1,128)S(1)} %add.9), channel_id=1, source_target_pairs={{0,18},{1,19},{2,16},{3,17},{4,22},{5,23},{6,20},{7,21},{8,26},{9,... | collective-permute-start | bytes 6152 | tf_op jit(solution)/shard_map/ppermute | solution.py:356
  51.4 2.6 %collective-permute-done.3 = f32[1,512]{1,0:T(1,128)S(1)} collective-permute-done((f32[1,512]{1,0:T(1,128)S(1)}, f32[1,512]{1,0:T(1,128)S(1)}, u32[]{:S(2)}, u32[]{:S(2)}) %collective-permute-start.3) | collective-permute-done | bytes 2080 | tf_op jit(solution)/shard_map/ppermute | solution.py:356
  54.0 0.0 collective-permute-start.4
  54.0 3.6 %collective-permute-done.4 = f32[1,512]{1,0:T(1,128)S(1)} collective-permute-done((f32[1,512]{1,0:T(1,128)S(1)}, f32[1,512]{1,0:T(1,128)S(1)}, u32[]{:S(2)}, u32[]{:S(2)}) %collective-permute-start.4) | collective-permute-done | bytes 2080 | tf_op jit(solution)/shard_map/ppermute | solution.py:357
  57.6 0.0 collective-permute-done.1.other_ref
  57.6 0.0 copy-done
  57.6 1.0 %shard_map.72 = (f32[2,32,64]{2,1,0:T(8,128)}, f32[2,16,32]{2,1,0:T(8,128)}) custom-call(f32[64,512]{1,0:T(8,128)S(1)} %shard_map.71.own_ref, f32[64,512]{1,0:T(8,128)S(1)} %collective-permute-done.1.other_ref, f32[1,512]{1,0:T(1,128)S(1)} %add.11.diag_ref, f32[2,64,512]{2,1,0:T(8,128)S(1)} %bitcast.16, s32[1,16]{1,0:T(1,128)S(1)} %get-tuple-element.19.order_ref), custom_call_target="tpu_custom_call" | custom-call | tf_op jit(solution)/shard_map/pallas_call | solution.py:358
  (7 shorter events, 0.2 us)
Async XLA Ops:
  1.7 5.6 %collective-permute-start = (f32[72,512]{1,0:T(8,128)S(1)}, f32[72,512]{1,0:T(8,128)S(1)}, u32[]{:S(2)}, u32[]{:S(2)}) collective-permute-start(f32[72,512]{1,0:T(8,128)S(1)} %get-tuple-element.13), channel_id=1, source_target_pairs={{0,16},{4,20},{8,24},{12,28},{16,0},{20,4},{24,8},{28,12},{32,48},... | collective-permute-start | bytes 442376 | tf_op jit(solution)/shard_map/ppermute | solution.py:332
  41.1 4.0 %copy-start.1 = (f32[2,32,512]{2,1,0:T(8,128)S(1)}, f32[2,32,512]{2,1,0:T(8,128)}, u32[]{:S(2)}) copy-start(f32[2,32,512]{2,1,0:T(8,128)} %downlink_ref.1) | copy-start | bytes 393220
  45.1 12.5 %copy-start = (f32[2,1,64,512]{3,2,1,0:T(8,128)S(1)}, f32[2,1,64,512]{3,2,1,0:T(8,128)}, u32[]{:S(2)}) copy-start(f32[2,1,64,512]{3,2,1,0:T(8,128)} %param.5) | copy-start | bytes 786436
  46.4 11.2 %collective-permute-start.1 = (f32[64,512]{1,0:T(8,128)S(1)}, f32[64,512]{1,0:T(8,128)S(1)}, u32[]{:S(2)}, u32[]{:S(2)}) collective-permute-start(f32[64,512]{1,0:T(8,128)S(1)} %shard_map.71.own_ref), channel_id=1, source_target_pairs={{0,16},{4,20},{8,24},{12,28},{16,0},{20,4},{24,8},{28,12},{32,48},... | collective-permute-start | bytes 393224 | tf_op jit(solution)/shard_map/ppermute | solution.py:354
  48.1 1.2 %collective-permute-start.2 = (f32[1,512]{1,0:T(1,128)S(1)}, f32[1,512]{1,0:T(1,128)S(1)}, u32[]{:S(2)}, u32[]{:S(2)}) collective-permute-start(f32[1,512]{1,0:T(1,128)S(1)} %get-tuple-element.18), channel_id=1, source_target_pairs={{0,1},{1,0},{2,3},{3,2},{4,5},{5,4},{6,7},{7,6},{8,9},{9,8},{10,11... | collective-permute-start | bytes 6152 | tf_op jit(solution)/shard_map/ppermute | solution.py:355
  49.2 4.8 %collective-permute-start.3 = (f32[1,512]{1,0:T(1,128)S(1)}, f32[1,512]{1,0:T(1,128)S(1)}, u32[]{:S(2)}, u32[]{:S(2)}) collective-permute-start(f32[1,512]{1,0:T(1,128)S(1)} %add.9), channel_id=1, source_target_pairs={{0,18},{1,19},{2,16},{3,17},{4,22},{5,23},{6,20},{7,21},{8,26},{9,... | collective-permute-start | bytes 6152 | tf_op jit(solution)/shard_map/ppermute | solution.py:356
  54.0 3.6 %collective-permute-start.4 = (f32[1,512]{1,0:T(1,128)S(1)}, f32[1,512]{1,0:T(1,128)S(1)}, u32[]{:S(2)}, u32[]{:S(2)}) collective-permute-start(f32[1,512]{1,0:T(1,128)S(1)} %add.10), channel_id=1, source_target_pairs={{0,16},{4,20},{8,24},{12,28},{16,0},{20,4},{24,8},{28,12},{32,48},... | collective-permute-start | bytes 6152 | tf_op jit(solution)/shard_map/ppermute | solution.py:357

commit v4 on v3

--- a/solution.py
+++ b/solution.py
@@ -54,23 +54,21 @@
         copy.wait()
 
 
-def gram(symbols, keep_ref, take_ref, out_ref):
-    antennas, users = keep_ref.shape[0] - 8, keep_ref.shape[1]
-
-    def scaled(ref):
-        extra = ref[antennas:]
-        scale = 1.0 / jnp.sqrt(extra[:1, antennas : antennas + 1])
-        chunks = [extra[:, k * TILE : k * TILE + antennas] for k in range(symbols // 8)]
-        return ref[:antennas] * scale, jnp.concatenate(chunks, axis=0) * scale
-
-    own, own_samples = scaled(keep_ref)
-    other, other_samples = scaled(take_ref)
-    both = jnp.concatenate([own, other], axis=0)
-    samples = jnp.concatenate([own_samples, other_samples], axis=1)
-    high, low = split(both)
+def gram(symbols, block_ref, *rest):
+    *base, out_ref = rest
+    antennas, users = block_ref.shape[0] - 8, block_ref.shape[1]
+
+    def put(at, value):
+        rows = slice(at, at + value.shape[0])
+        out_ref[rows] = base[0][rows] + value if base else value
+
+    extra = block_ref[antennas:]
+    scale = 1.0 / jnp.sqrt(extra[:1, antennas : antennas + 1])
+    samples = jnp.concatenate([extra[:, k * TILE : k * TILE + antennas] for k in range(symbols // 8)], axis=0)
+    high, low = split(block_ref[:antennas] * scale)
     left = jnp.concatenate([high, high, low], axis=0).T
     right = jnp.concatenate([high, low, high], axis=0)
-    y_high, y_low = split(samples)
+    y_high, y_low = split(samples * scale)
     mixed = mm(jnp.concatenate([y_high, y_high, y_low], axis=1), right)
     tiles, at = users // TILE, 0
     lower = lower_of(TILE)
@@ -78,19 +76,19 @@
     for i in range(tiles):
         row = mm(left[i * TILE : (i + 1) * TILE], right[:, : (i + 1) * TILE])
         for j in range(i):
-            out_ref[at : at + TILE] = row[:, j * TILE : (j + 1) * TILE]
+            put(at, row[:, j * TILE : (j + 1) * TILE])
             at += TILE
         diagonal.append(row[:, i * TILE :])
     for i in range(0, tiles, 2):
-        out_ref[at : at + TILE] = jnp.where(lower, diagonal[i], diagonal[i + 1])
+        put(at, jnp.where(lower, diagonal[i], diagonal[i + 1]))
         at += TILE
     for j in range(tiles):
-        out_ref[at : at + symbols] = mixed[:, j * TILE : (j + 1) * TILE]
+        put(at, mixed[:, j * TILE : (j + 1) * TILE])
         at += symbols
-    out_ref[at:] = jnp.zeros((out_ref.shape[0] - at, TILE), F32)
-    for i in range(1, tiles, 2):
-        out_ref[at : at + 1] = jnp.sum(jnp.where(eye_of(TILE), diagonal[i], 0.0), axis=0, keepdims=True)
-        at += 1
+    ends = [
+        jnp.sum(jnp.where(eye_of(TILE), diagonal[i], 0.0), axis=0, keepdims=True) for i in range(1, tiles, 2)
+    ]
+    put(at, jnp.concatenate(ends + [jnp.zeros((out_ref.shape[0] - at - len(ends), TILE), F32)], axis=0))
 
 
 def lower_of(n):
@@ -165,16 +163,24 @@
     x = (gain_of(bound) * (x.astype(F32) + mm(x, s_ref[:n]))).astype(BF16)
     x_ref[...] = x
     a_high, a_low = split(a_ref[...])
-    parts = mm(jnp.concatenate([a_high, a_low], axis=0), x)
-    error = eye - (parts[:n] + parts[n:])
-    e = error.astype(BF16)
-    e_ref[...] = e
-    both = mm(jnp.concatenate([e, x], axis=0), e)
-    twice, update = both[:n], both[n:]
-    v_ref[...] = twice.astype(BF16)
-    diag = jnp.where(eye_of(n), x.astype(F32) + update, 0.0) + (error + twice) * update
-    diag_ref[...] = jnp.sum(diag, axis=0, keepdims=True)
-    good = jnp.sum(twice * twice) < 3e-5
+    strips = [slice(at, at + 128) for at in range(0, n, 128)]
+    parts = mm(jnp.concatenate([part for rows in strips for part in (a_high[rows], a_low[rows])], axis=0), x)
+    for k, rows in enumerate(strips):
+        product = parts[2 * k * 128 : (2 * k + 1) * 128] + parts[(2 * k + 1) * 128 : (2 * k + 2) * 128]
+        e_ref[rows] = (eye[rows] - product).astype(BF16)
+    e = e_ref[...]
+    blocks = [slice(at, at + 128) for at in range(0, n, 128)]
+    both = mm(jnp.concatenate([part for rows in blocks for part in (e[rows], x[rows])], axis=0), e)
+    diag, size = jnp.zeros((1, n), F32), jnp.zeros((1, n), F32)
+    for k, rows in enumerate(blocks):
+        twice = both[2 * k * 128 : (2 * k + 1) * 128]
+        update = both[(2 * k + 1) * 128 : (2 * k + 2) * 128]
+        v_ref[rows] = twice.astype(BF16)
+        own = jnp.where(eye[rows] > 0.0, x[rows].astype(F32) + update, 0.0)
+        diag = diag + jnp.sum(own + (e[rows].astype(F32) + twice) * update, axis=0, keepdims=True)
+        size = size + jnp.sum(twice * twice, axis=0, keepdims=True)
+    diag_ref[...] = diag
+    good = jnp.sum(size) < 3e-5
     flag_ref[0] = good.astype(jnp.int32)
 
     @pl.when(jnp.logical_not(good))
@@ -329,11 +335,12 @@
         [pltpu.VMEM(received.shape, F32), pltpu.SMEM((blocks,), F32), pltpu.SemaphoreType.DMA((5,))],
         8 << 20,
     )(outside(channel), outside(received), outside(noise_var), outside(order))
-    take = lax.ppermute(give, "stripe", swap)
     tiles, group = n // TILE, len(planes[0])
     used = tiles * tiles // 2 * TILE + tiles * symbols + tiles // 2
     height = -(-used // group) * group
-    part = call(functools.partial(gram, symbols), struct(height, TILE), [VMEM, VMEM])(keep, take)
+    take = lax.ppermute(give, "stripe", swap)
+    own = call(functools.partial(gram, symbols), struct(height, TILE), [VMEM], flops=10**9)(keep)
+    part = call(functools.partial(gram, symbols), struct(height, TILE), [VMEM, VMEM])(take, own)
     part = part.reshape(height, 1, TILE)
     part = lax.all_to_all(part, "stripe", 0, 0, axis_index_groups=planes, tiled=True)
     part = lax.optimization_barrier(part.reshape(height, TILE))

time: 58.8 us -> 58.6 us (level)
  transfers between devices with their start and end apart: 5 -> 5, of which waited for: 4 -> 4; matrix products, arithmetic and copies ran while one was open for 0% -> 0% of each run, Pallas kernels for 0% -> 1%
where the time goes in v4:
time: 58.6 us; the launch traced here: 58.4 us
  blocking collectives  33 us (56%)
  waiting for transfers between devices  10.8 us (18%)
  Pallas kernels  8.09 us (14%)
  starting transfers between devices  5.59 us (10%)
  between operations  0.73 us (1%)
    all_to_all x2, blocking collectives, shards(): lax.all_to_all(part, 'stripe', 0, 0, axis_index_groups=planes, tiled=True)  33 us
    pallas_call x1, Pallas kernels, shards(): call(functools.partial(invert, symbols), (struct(1, n), jax.ShapeDtypeStr...  3.89 us
    ppermute x1, waiting for transfers between devices, shards(): diag = diag + lax.ppermute(diag, 'stripe', swap)  3.58 us
    ppermute x1, waiting for transfers between devices, shards(): take = lax.ppermute(give, 'stripe', swap)  3.38 us
    ppermute x1, waiting for transfers between devices, shards(): diag = diag + lax.ppermute(diag, ('stripe', 'sub'), across)  2.64 us
    ppermute x1, starting transfers between devices, shards(): diag = diag + lax.ppermute(diag, ('stripe', 'sub'), across)  2.16 us
    ppermute x1, starting transfers between devices, shards(): take = lax.ppermute(give, 'stripe', swap)  1.77 us
    ppermute x1, starting transfers between devices, shards(): other = lax.ppermute(rows, 'stripe', swap)  1.66 us
  transfers between devices with their start and end apart: 5, of which 4 were waited for; matrix products, arithmetic and copies ran while one was open for 0% of the time, Pallas kernels for 1%

profile of v4, /device:TPU:0, one launch (start us, length us, event | category | flops | bytes accessed | tf_op | source)
XLA Modules:
  0.0 58.4 jit_solution(10536031075838545210)
XLA Ops:
  0.6 1.0 %shard_map.68 = (f32[72,512]{1,0:T(8,128)S(1)}, f32[72,512]{1,0:T(8,128)S(1)}, s32[1,16]{1,0:T(1,128)S(1)}) custom-call(f32[2,64,512]{2,1,0:T(8,128)} %bitcast.15, f32[2,32,64]{2,1,0:T(8,128)} %received_ref.1, f32[2]{0:T(128)} %bitcast.19, s32[1,16]{1,0:T(1,128)} %bitcast.20), custom_call_target="tpu_custom_call" | custom-call | tf_op jit(solution)/shard_map/pallas_call | solution.py:331
  1.7 1.8 %collective-permute-start = (f32[72,512]{1,0:T(8,128)S(1)}, f32[72,512]{1,0:T(8,128)S(1)}, u32[]{:S(2)}, u32[]{:S(2)}) collective-permute-start(f32[72,512]{1,0:T(8,128)S(1)} %get-tuple-element.12), channel_id=1, source_target_pairs={{0,16},{4,20},{8,24},{12,28},{16,0},{20,4},{24,8},{28,12},{32,48},... | collective-permute-start | bytes 442376 | tf_op jit(solution)/shard_map/ppermute | solution.py:341
  3.5 0.5 shard_map.69.rest_0_
  3.9 3.4 %collective-permute-done.block_ref = f32[72,512]{1,0:T(8,128)S(1)} collective-permute-done((f32[72,512]{1,0:T(8,128)S(1)}, f32[72,512]{1,0:T(8,128)S(1)}, u32[]{:S(2)}, u32[]{:S(2)}) %collective-permute-start) | collective-permute-done | bytes 147488 | tf_op jit(solution)/shard_map/ppermute | solution.py:341
  7.3 0.5 shard_map.70
  7.8 19.3 %all_to_all.10 = f32[1168,1,128]{2,1,0:T(1,128)S(1)} all-to-all(f32[1168,1,128]{2,1,0:T(1,128)S(1)} %bitcast.14), channel_id=1, replica_groups={{0,4,8,12,32,36,40,44,64,68,72,76,96,100,104,108},{16,20,24,28,48,52,56..., dimensions={0} | all-to-all | bytes 1196032 | tf_op jit(solution)/shard_map/all_to_all | solution.py:345
  27.2 13.7 %all_to_all.11 = f32[1168,1,128]{2,1,0:T(1,128)S(1)} all-to-all(f32[1168,1,128]{2,1,0:T(1,128)S(1)} %bitcast.18), channel_id=1, replica_groups={{0,4,8,12,32,36,40,44,64,68,72,76,96,100,104,108},{16,20,24,28,48,52,56..., dimensions={0} | all-to-all | bytes 1196032 | tf_op jit(solution)/shard_map/all_to_all | solution.py:350
  41.0 0.0 copy-start.1
  41.0 3.9 %shard_map.71 = (f32[1,512]{1,0:T(1,128)S(1)}, s32[1]{0:T(128)}, bf16[512,512]{1,0:T(8,128)(2,1)S(1)}, bf16[512,512]{1,0:T(8,128)(2,1)S(1)}, bf16[512,512]{1,0:T(8,128)(2,1)S(1)}) custom-call(f32[1168,128]{1,0:T(8,128)S(1)} %bitcast.12), custom_call_target="tpu_custom_call" | custom-call | tf_op jit(solution)/shard_map/pallas_call | solution.py:353
  44.9 0.0 copy-done.1
  44.9 0.0 copy-start
  44.9 1.3 %shard_map.72.own_ref = f32[64,512]{1,0:T(8,128)S(1)} custom-call(s32[1]{0:T(128)} %get-tuple-element.14.flag_ref, f32[1168,128]{1,0:T(8,128)S(1)} %bitcast.13, f32[2,32,512]{2,1,0:T(8,128)S(1)} %copy-done.1, bf16[512,512]{1,0:T(8,128)(2,1)S(1)} %get-tuple-element.15.x_ref, bf16[512,512]{1,0:T(8,128)(2,1)S(1)} %get-tuple-element.16.e_ref, ...), custom_call_target="tpu_custom_call" | custom-call | flops 1000000000 | bytes 2097152 | tf_op jit(solution)/shard_map/pallas_call | solution.py:360
  46.2 1.7 %collective-permute-start.1 = (f32[64,512]{1,0:T(8,128)S(1)}, f32[64,512]{1,0:T(8,128)S(1)}, u32[]{:S(2)}, u32[]{:S(2)}) collective-permute-start(f32[64,512]{1,0:T(8,128)S(1)} %shard_map.72.own_ref), channel_id=1, source_target_pairs={{0,16},{4,20},{8,24},{12,28},{16,0},{20,4},{24,8},{28,12},{32,48},... | collective-permute-start | bytes 393224 | tf_op jit(solution)/shard_map/ppermute | solution.py:361
  47.8 0.0 collective-permute-start.2
  47.8 1.2 %collective-permute-done.2 = f32[1,512]{1,0:T(1,128)S(1)} collective-permute-done((f32[1,512]{1,0:T(1,128)S(1)}, f32[1,512]{1,0:T(1,128)S(1)}, u32[]{:S(2)}, u32[]{:S(2)}) %collective-permute-start.2) | collective-permute-done | bytes 2080 | tf_op jit(solution)/shard_map/ppermute | solution.py:362
  49.0 2.2 %collective-permute-start.3 = (f32[1,512]{1,0:T(1,128)S(1)}, f32[1,512]{1,0:T(1,128)S(1)}, u32[]{:S(2)}, u32[]{:S(2)}) collective-permute-start(f32[1,512]{1,0:T(1,128)S(1)} %add.9), channel_id=1, source_target_pairs={{0,18},{1,19},{2,16},{3,17},{4,22},{5,23},{6,20},{7,21},{8,26},{9,... | collective-permute-start | bytes 6152 | tf_op jit(solution)/shard_map/ppermute | solution.py:363
  51.2 2.6 %collective-permute-done.3 = f32[1,512]{1,0:T(1,128)S(1)} collective-permute-done((f32[1,512]{1,0:T(1,128)S(1)}, f32[1,512]{1,0:T(1,128)S(1)}, u32[]{:S(2)}, u32[]{:S(2)}) %collective-permute-start.3) | collective-permute-done | bytes 2080 | tf_op jit(solution)/shard_map/ppermute | solution.py:363
  53.8 0.0 collective-permute-start.4
  53.8 3.6 %collective-permute-done.4 = f32[1,512]{1,0:T(1,128)S(1)} collective-permute-done((f32[1,512]{1,0:T(1,128)S(1)}, f32[1,512]{1,0:T(1,128)S(1)}, u32[]{:S(2)}, u32[]{:S(2)}) %collective-permute-start.4) | collective-permute-done | bytes 2080 | tf_op jit(solution)/shard_map/ppermute | solution.py:364
  57.4 0.0 collective-permute-done.1.other_ref
  57.4 0.0 copy-done
  57.4 1.0 %shard_map.73 = (f32[2,32,64]{2,1,0:T(8,128)}, f32[2,16,32]{2,1,0:T(8,128)}) custom-call(f32[64,512]{1,0:T(8,128)S(1)} %shard_map.72.own_ref, f32[64,512]{1,0:T(8,128)S(1)} %collective-permute-done.1.other_ref, f32[1,512]{1,0:T(1,128)S(1)} %add.11.diag_ref, f32[2,64,512]{2,1,0:T(8,128)S(1)} %bitcast.16, s32[1,16]{1,0:T(1,128)S(1)} %get-tuple-element.19.order_ref), custom_call_target="tpu_custom_call" | custom-call | tf_op jit(solution)/shard_map/pallas_call | solution.py:365
  (7 shorter events, 0.2 us)
Async XLA Ops:
  1.7 5.6 %collective-permute-start = (f32[72,512]{1,0:T(8,128)S(1)}, f32[72,512]{1,0:T(8,128)S(1)}, u32[]{:S(2)}, u32[]{:S(2)}) collective-permute-start(f32[72,512]{1,0:T(8,128)S(1)} %get-tuple-element.12), channel_id=1, source_target_pairs={{0,16},{4,20},{8,24},{12,28},{16,0},{20,4},{24,8},{28,12},{32,48},... | collective-permute-start | bytes 442376 | tf_op jit(solution)/shard_map/ppermute | solution.py:341
  41.0 3.9 %copy-start.1 = (f32[2,32,512]{2,1,0:T(8,128)S(1)}, f32[2,32,512]{2,1,0:T(8,128)}, u32[]{:S(2)}) copy-start(f32[2,32,512]{2,1,0:T(8,128)} %downlink_ref.1) | copy-start | bytes 393220
  44.9 12.5 %copy-start = (f32[2,1,64,512]{3,2,1,0:T(8,128)S(1)}, f32[2,1,64,512]{3,2,1,0:T(8,128)}, u32[]{:S(2)}) copy-start(f32[2,1,64,512]{3,2,1,0:T(8,128)} %param.5) | copy-start | bytes 786436
  46.2 11.2 %collective-permute-start.1 = (f32[64,512]{1,0:T(8,128)S(1)}, f32[64,512]{1,0:T(8,128)S(1)}, u32[]{:S(2)}, u32[]{:S(2)}) collective-permute-start(f32[64,512]{1,0:T(8,128)S(1)} %shard_map.72.own_ref), channel_id=1, source_target_pairs={{0,16},{4,20},{8,24},{12,28},{16,0},{20,4},{24,8},{28,12},{32,48},... | collective-permute-start | bytes 393224 | tf_op jit(solution)/shard_map/ppermute | solution.py:361
  47.8 1.2 %collective-permute-start.2 = (f32[1,512]{1,0:T(1,128)S(1)}, f32[1,512]{1,0:T(1,128)S(1)}, u32[]{:S(2)}, u32[]{:S(2)}) collective-permute-start(f32[1,512]{1,0:T(1,128)S(1)} %get-tuple-element.18), channel_id=1, source_target_pairs={{0,1},{1,0},{2,3},{3,2},{4,5},{5,4},{6,7},{7,6},{8,9},{9,8},{10,11... | collective-permute-start | bytes 6152 | tf_op jit(solution)/shard_map/ppermute | solution.py:362
  49.0 4.8 %collective-permute-start.3 = (f32[1,512]{1,0:T(1,128)S(1)}, f32[1,512]{1,0:T(1,128)S(1)}, u32[]{:S(2)}, u32[]{:S(2)}) collective-permute-start(f32[1,512]{1,0:T(1,128)S(1)} %add.9), channel_id=1, source_target_pairs={{0,18},{1,19},{2,16},{3,17},{4,22},{5,23},{6,20},{7,21},{8,26},{9,... | collective-permute-start | bytes 6152 | tf_op jit(solution)/shard_map/ppermute | solution.py:363
  53.8 3.6 %collective-permute-start.4 = (f32[1,512]{1,0:T(1,128)S(1)}, f32[1,512]{1,0:T(1,128)S(1)}, u32[]{:S(2)}, u32[]{:S(2)}) collective-permute-start(f32[1,512]{1,0:T(1,128)S(1)} %add.10), channel_id=1, source_target_pairs={{0,16},{4,20},{8,24},{12,28},{16,0},{20,4},{24,8},{28,12},{32,48},... | collective-permute-start | bytes 6152 | tf_op jit(solution)/shard_map/ppermute | solution.py:364

commit v5 on v4

--- a/solution.py
+++ b/solution.py
@@ -44,14 +44,19 @@
     ]
     for copy in copies:
         copy.start()
-    for copy in copies[:2]:
+    for copy in copies[:3]:
         copy.wait()
     for which, out_ref in sides:
         out_ref[antennas:] = jnp.full((8, out_ref.shape[1]), noise[which], F32)
         for k in range(samples.shape[1] // 8):
             out_ref[antennas:, k * TILE : k * TILE + antennas] = samples[which, 8 * k : 8 * k + 8]
-    for copy in copies[2:]:
+    give_ref[antennas : antennas + 1, order_lanes(antennas, order_ref.shape[1])] = kept_ref[...].astype(F32)
+    for copy in copies[3:]:
         copy.wait()
+
+
+def order_lanes(antennas, count):
+    return slice(TILE + antennas, TILE + antennas + count)
 
 
 def gram(symbols, block_ref, *rest):
@@ -136,15 +141,18 @@
     top = jnp.max(jnp.sum(jnp.abs(a), axis=0, keepdims=True), axis=1, keepdims=True) * 1.0001
     alpha = 2.0 / (prior + top)
     start = (top - prior) / (top + prior)
-    left = (eye - alpha * a).astype(BF16)
-    s_ref[n:] = ((alpha * gain_of(start)) * (eye + left.astype(F32))).astype(BF16)
+    a_high, a_low = split(a)
+    rounded = a_high.astype(F32)
+    gain = alpha * gain_of(start)
+    s_ref[n:] = ((2.0 * gain) * eye - (gain * alpha) * rounded).astype(BF16)
 
     def squared(product, bound):
         square = bound * bound
         scale = 1.0 / (2.0 - square)
         return ((2.0 * scale) * product - (square * scale) * eye).astype(BF16)
 
-    s_ref[:n] = squared(mm(left, left), start)
+    scale = 2.0 * alpha / (2.0 - start * start)
+    s_ref[:n] = (eye + (scale * alpha) * mm(a_high, a_high) - (2.0 * scale) * rounded).astype(BF16)
     first = after(start)
     bound, steps = first, jnp.zeros((1, 1), F32)
     for _ in range(10):
@@ -162,7 +170,6 @@
     x = s_ref[n:]
     x = (gain_of(bound) * (x.astype(F32) + mm(x, s_ref[:n]))).astype(BF16)
     x_ref[...] = x
-    a_high, a_low = split(a_ref[...])
     strips = [slice(at, at + 128) for at in range(0, n, 128)]
     parts = mm(jnp.concatenate([part for rows in strips for part in (a_high[rows], a_low[rows])], axis=0), x)
     for k, rows in enumerate(strips):
@@ -265,29 +272,40 @@
         rows_ref[...] = exact(rows, x)
 
 
-def finish(terms, own_ref, other_ref, diag_ref, channel_ref, order_ref, transmit_ref, owned_ref):
+def claim(symbols, rows_ref, order_ref, take_ref, give_ref, owned_ref):
+    n, count = rows_ref.shape[1], order_ref.shape[1]
+    antennas = take_ref.shape[0] - 8
+    theirs = take_ref[antennas : antennas + 1, order_lanes(antennas, count)].astype(jnp.int32)
+    order = jnp.concatenate([order_ref[...], theirs], axis=1)
+    pick = (lax.broadcasted_iota(jnp.int32, (n, 2 * count), 0) == order).astype(BF16)
+    x = rows_ref[symbols:]
+    high = x.astype(BF16)
+    middle, low = split(x - high.astype(F32))
+    parts = mm(jnp.concatenate([high, middle, low], axis=0), pick)
+    picked = (parts[:symbols] + (parts[symbols : 2 * symbols] + parts[2 * symbols :])).T
+    owned_ref[...] = picked[:count]
+    give_ref[:symbols] = rows_ref[:symbols]
+    give_ref[symbols:] = jnp.zeros((8, n), F32)
+    for k in range(count // 8):
+        give_ref[symbols:, k * TILE : k * TILE + symbols] = picked[count + 8 * k : count + 8 * k + 8]
+
+
+def finish(terms, own_ref, other_ref, mine_ref, diag_ref, channel_ref, transmit_ref, owned_ref):
     mine = kept_block()
-    blocks, symbols = transmit_ref.shape[0], transmit_ref.shape[1]
+    symbols, count = transmit_ref.shape[1], owned_ref.shape[1]
     mean_error = diag_ref[...] / terms
     scale = lax.rsqrt(mean_error)
     scale = scale * (1.5 - 0.5 * mean_error * scale * scale)
-    n = own_ref.shape[1]
-    order = order_ref[...]
-    pick = (lax.broadcasted_iota(jnp.int32, (n, order.shape[1]), 0) == order).astype(BF16)
-    for block in range(blocks):
-        z = jnp.where(mine == block, own_ref[...], other_ref[...])
-        high, low = split(z[:symbols] * scale)
+    for block, rows_ref in ((mine, own_ref), (1 - mine, other_ref)):
+        high, low = split(rows_ref[:symbols] * scale)
         h_high, h_low = split(channel_ref[block])
         left = jnp.concatenate([high, low], axis=0)
         one = mm(left, h_high, ((1,), (1,)))
         two = mm(high, h_low, ((1,), (1,)))
         transmit_ref[block] = one[:symbols] + (one[symbols:] + two)
-        x = z[symbols:]
-        high = x.astype(BF16)
-        rest = x - high.astype(F32)
-        middle, low = split(rest)
-        parts = mm(jnp.concatenate([high, middle, low], axis=0), pick)
-        owned_ref[block] = (parts[:symbols] + (parts[symbols : 2 * symbols] + parts[2 * symbols :])).T
+    owned_ref[mine] = mine_ref[...]
+    theirs = [other_ref[symbols:, k * TILE : k * TILE + symbols] for k in range(count // 8)]
+    owned_ref[1 - mine] = jnp.concatenate(theirs, axis=0)
 
 
 VMEM = pl.BlockSpec(memory_space=pltpu.VMEM)
@@ -358,7 +376,13 @@
         outs_in=(VMEM, SMEM, VMEM, VMEM, VMEM),
     )(whole)
     rows = call(apply, struct(2 * symbols, n), [SMEM] + [VMEM] * 5, flops=10**9)(flag, whole, downlink, x, e, v)
-    other = lax.ppermute(rows, "stripe", swap)
+    claimed, picked = call(
+        functools.partial(claim, symbols),
+        (struct(symbols + 8, n), struct(order.shape[1], symbols)),
+        [VMEM] * 3,
+        flops=10**8,
+    )(rows, order, take)
+    other = lax.ppermute(claimed, "stripe", swap)
     diag = diag + lax.ppermute(diag, "sub", cores)
     diag = diag + lax.ppermute(diag, ("stripe", "sub"), across)
     diag = diag + lax.ppermute(diag, "stripe", swap)
@@ -366,7 +390,7 @@
         functools.partial(finish, blocks * subs),
         (struct(blocks, symbols, antennas), struct(blocks, order.shape[1], symbols)),
         [VMEM] * 5,
-    )(rows, other, diag, channel, order)
+    )(rows, other, picked, diag, channel)
     return transmit, owned.transpose(0, 2, 1)
 
 

time: 58.6 us -> 58.5 us (level)
  no operation moved by 1% of the time
where the time goes in v5:
time: 58.5 us; the launch traced here: 58.3 us
  blocking collectives  33 us (56%)
  waiting for transfers between devices  10.7 us (18%)
  Pallas kernels  8.08 us (14%)
  starting transfers between devices  5.54 us (9%)
  between operations  0.73 us (1%)
    all_to_all x2, blocking collectives, shards(): lax.all_to_all(part, 'stripe', 0, 0, axis_index_groups=planes, tiled=True)  33 us
    pallas_call x1, Pallas kernels, shards(): call(functools.partial(invert, symbols), (struct(1, n), jax.ShapeDtypeStr...  3.74 us
    ppermute x1, waiting for transfers between devices, shards(): diag = diag + lax.ppermute(diag, 'stripe', swap)  3.58 us
    ppermute x1, waiting for transfers between devices, shards(): take = lax.ppermute(give, 'stripe', swap)  3.38 us
    ppermute x1, waiting for transfers between devices, shards(): diag = diag + lax.ppermute(diag, ('stripe', 'sub'), across)  2.62 us
    ppermute x1, starting transfers between devices, shards(): diag = diag + lax.ppermute(diag, ('stripe', 'sub'), across)  2.17 us
    ppermute x1, starting transfers between devices, shards(): take = lax.ppermute(give, 'stripe', swap)  1.77 us
    ppermute x1, starting transfers between devices, shards(): other = lax.ppermute(claimed, 'stripe', swap)  1.59 us
  transfers between devices with their start and end apart: 5, of which 4 were waited for; matrix products, arithmetic and copies ran while one was open for 0% of the time, Pallas kernels for 1%

profile of v5, /device:TPU:0, one launch (start us, length us, event | category | flops | bytes accessed | tf_op | source)
XLA Modules:
  0.0 58.3 jit_solution(1646361556498352906)
XLA Ops:
  0.6 1.0 %shard_map.68 = (f32[72,512]{1,0:T(8,128)S(1)}, f32[72,512]{1,0:T(8,128)S(1)}, s32[1,16]{1,0:T(1,128)S(1)}) custom-call(f32[2,64,512]{2,1,0:T(8,128)} %bitcast.15, f32[2,32,64]{2,1,0:T(8,128)} %received_ref.1, f32[2]{0:T(128)} %bitcast.19, s32[1,16]{1,0:T(1,128)} %bitcast.20), custom_call_target="tpu_custom_call" | custom-call | tf_op jit(solution)/shard_map/pallas_call | solution.py:349
  1.7 1.8 %collective-permute-start = (f32[72,512]{1,0:T(8,128)S(1)}, f32[72,512]{1,0:T(8,128)S(1)}, u32[]{:S(2)}, u32[]{:S(2)}) collective-permute-start(f32[72,512]{1,0:T(8,128)S(1)} %get-tuple-element.14), channel_id=1, source_target_pairs={{0,16},{4,20},{8,24},{12,28},{16,0},{20,4},{24,8},{28,12},{32,48},... | collective-permute-start | bytes 442376 | tf_op jit(solution)/shard_map/ppermute | solution.py:359
  3.5 0.5 shard_map.69.rest_0_
  3.9 3.4 %collective-permute-done.block_ref.take_ref = f32[72,512]{1,0:T(8,128)S(1)} collective-permute-done((f32[72,512]{1,0:T(8,128)S(1)}, f32[72,512]{1,0:T(8,128)S(1)}, u32[]{:S(2)}, u32[]{:S(2)}) %collective-permute-start) | collective-permute-done | bytes 147488 | tf_op jit(solution)/shard_map/ppermute | solution.py:359
  7.3 0.5 shard_map.70
  7.8 19.3 %all_to_all.10 = f32[1168,1,128]{2,1,0:T(1,128)S(1)} all-to-all(f32[1168,1,128]{2,1,0:T(1,128)S(1)} %bitcast.14), channel_id=1, replica_groups={{0,4,8,12,32,36,40,44,64,68,72,76,96,100,104,108},{16,20,24,28,48,52,56..., dimensions={0} | all-to-all | bytes 1196032 | tf_op jit(solution)/shard_map/all_to_all | solution.py:363
  27.2 13.7 %all_to_all.11 = f32[1168,1,128]{2,1,0:T(1,128)S(1)} all-to-all(f32[1168,1,128]{2,1,0:T(1,128)S(1)} %bitcast.18), channel_id=1, replica_groups={{0,4,8,12,32,36,40,44,64,68,72,76,96,100,104,108},{16,20,24,28,48,52,56..., dimensions={0} | all-to-all | bytes 1196032 | tf_op jit(solution)/shard_map/all_to_all | solution.py:368
  41.0 0.0 copy-start.1
  41.0 3.7 %shard_map.71 = (f32[1,512]{1,0:T(1,128)S(1)}, s32[1]{0:T(128)}, bf16[512,512]{1,0:T(8,128)(2,1)S(1)}, bf16[512,512]{1,0:T(8,128)(2,1)S(1)}, bf16[512,512]{1,0:T(8,128)(2,1)S(1)}) custom-call(f32[1168,128]{1,0:T(8,128)S(1)} %bitcast.12), custom_call_target="tpu_custom_call" | custom-call | tf_op jit(solution)/shard_map/pallas_call | solution.py:371
  44.7 0.0 copy-done.1
  44.7 1.2 %shard_map.72.rows_ref.own_ref = f32[64,512]{1,0:T(8,128)S(1)} custom-call(s32[1]{0:T(128)} %get-tuple-element.16.flag_ref, f32[1168,128]{1,0:T(8,128)S(1)} %bitcast.13, f32[2,32,512]{2,1,0:T(8,128)S(1)} %copy-done.1, bf16[512,512]{1,0:T(8,128)(2,1)S(1)} %get-tuple-element.17.x_ref, bf16[512,512]{1,0:T(8,128)(2,1)S(1)} %get-tuple-element.18.e_ref, ...), custom_call_target="tpu_custom_call" | custom-call | flops 1000000000 | bytes 2097152 | tf_op jit(solution)/shard_map/pallas_call | solution.py:378
  46.0 0.0 copy-start
  46.0 0.3 shard_map.73
  46.3 1.6 %collective-permute-start.1 = (f32[40,512]{1,0:T(8,128)S(1)}, f32[40,512]{1,0:T(8,128)S(1)}, u32[]{:S(2)}, u32[]{:S(2)}) collective-permute-start(f32[40,512]{1,0:T(8,128)S(1)} %get-tuple-element.21), channel_id=1, source_target_pairs={{0,16},{4,20},{8,24},{12,28},{16,0},{20,4},{24,8},{28,12},{32,48},... | collective-permute-start | bytes 245768 | tf_op jit(solution)/shard_map/ppermute | solution.py:385
  47.9 0.0 collective-permute-start.2
  47.9 1.2 %collective-permute-done.2 = f32[1,512]{1,0:T(1,128)S(1)} collective-permute-done((f32[1,512]{1,0:T(1,128)S(1)}, f32[1,512]{1,0:T(1,128)S(1)}, u32[]{:S(2)}, u32[]{:S(2)}) %collective-permute-start.2) | collective-permute-done | bytes 2080 | tf_op jit(solution)/shard_map/ppermute | solution.py:386
  49.1 2.2 %collective-permute-start.3 = (f32[1,512]{1,0:T(1,128)S(1)}, f32[1,512]{1,0:T(1,128)S(1)}, u32[]{:S(2)}, u32[]{:S(2)}) collective-permute-start(f32[1,512]{1,0:T(1,128)S(1)} %add.9), channel_id=1, source_target_pairs={{0,18},{1,19},{2,16},{3,17},{4,22},{5,23},{6,20},{7,21},{8,26},{9,... | collective-permute-start | bytes 6152 | tf_op jit(solution)/shard_map/ppermute | solution.py:387
  51.2 2.6 %collective-permute-done.3 = f32[1,512]{1,0:T(1,128)S(1)} collective-permute-done((f32[1,512]{1,0:T(1,128)S(1)}, f32[1,512]{1,0:T(1,128)S(1)}, u32[]{:S(2)}, u32[]{:S(2)}) %collective-permute-start.3) | collective-permute-done | bytes 2080 | tf_op jit(solution)/shard_map/ppermute | solution.py:387
  53.9 0.0 collective-permute-start.4
  53.9 3.6 %collective-permute-done.4 = f32[1,512]{1,0:T(1,128)S(1)} collective-permute-done((f32[1,512]{1,0:T(1,128)S(1)}, f32[1,512]{1,0:T(1,128)S(1)}, u32[]{:S(2)}, u32[]{:S(2)}) %collective-permute-start.4) | collective-permute-done | bytes 2080 | tf_op jit(solution)/shard_map/ppermute | solution.py:388
  57.4 0.0 collective-permute-done.1.other_ref
  57.4 0.0 copy-done
  57.5 0.8 %shard_map.74 = (f32[2,32,64]{2,1,0:T(8,128)}, f32[2,16,32]{2,1,0:T(8,128)}) custom-call(f32[64,512]{1,0:T(8,128)S(1)} %shard_map.72.rows_ref.own_ref, f32[40,512]{1,0:T(8,128)S(1)} %collective-permute-done.1.other_ref, f32[16,32]{1,0:T(8,128)S(1)} %get-tuple-element.22.mine_ref, f32[1,512]{1,0:T(1,128)S(1)} %add.11.diag_ref, f32[2,64,512]{2,1,0:T(8,128)S(1)} %bitcast.16), custom_call_target="tpu_custom_call" | custom-call | tf_op jit(solution)/shard_map/pallas_call | solution.py:389
  (7 shorter events, 0.2 us)
Async XLA Ops:
  1.7 5.6 %collective-permute-start = (f32[72,512]{1,0:T(8,128)S(1)}, f32[72,512]{1,0:T(8,128)S(1)}, u32[]{:S(2)}, u32[]{:S(2)}) collective-permute-start(f32[72,512]{1,0:T(8,128)S(1)} %get-tuple-element.14), channel_id=1, source_target_pairs={{0,16},{4,20},{8,24},{12,28},{16,0},{20,4},{24,8},{28,12},{32,48},... | collective-permute-start | bytes 442376 | tf_op jit(solution)/shard_map/ppermute | solution.py:359
  41.0 3.8 %copy-start.1 = (f32[2,32,512]{2,1,0:T(8,128)S(1)}, f32[2,32,512]{2,1,0:T(8,128)}, u32[]{:S(2)}) copy-start(f32[2,32,512]{2,1,0:T(8,128)} %downlink_ref.1) | copy-start | bytes 393220
  46.0 11.5 %copy-start = (f32[2,1,64,512]{3,2,1,0:T(8,128)S(1)}, f32[2,1,64,512]{3,2,1,0:T(8,128)}, u32[]{:S(2)}) copy-start(f32[2,1,64,512]{3,2,1,0:T(8,128)} %param.5) | copy-start | bytes 786436
  46.3 11.2 %collective-permute-start.1 = (f32[40,512]{1,0:T(8,128)S(1)}, f32[40,512]{1,0:T(8,128)S(1)}, u32[]{:S(2)}, u32[]{:S(2)}) collective-permute-start(f32[40,512]{1,0:T(8,128)S(1)} %get-tuple-element.21), channel_id=1, source_target_pairs={{0,16},{4,20},{8,24},{12,28},{16,0},{20,4},{24,8},{28,12},{32,48},... | collective-permute-start | bytes 245768 | tf_op jit(solution)/shard_map/ppermute | solution.py:385
  47.9 1.2 %collective-permute-start.2 = (f32[1,512]{1,0:T(1,128)S(1)}, f32[1,512]{1,0:T(1,128)S(1)}, u32[]{:S(2)}, u32[]{:S(2)}) collective-permute-start(f32[1,512]{1,0:T(1,128)S(1)} %get-tuple-element.23), channel_id=1, source_target_pairs={{0,1},{1,0},{2,3},{3,2},{4,5},{5,4},{6,7},{7,6},{8,9},{9,8},{10,11... | collective-permute-start | bytes 6152 | tf_op jit(solution)/shard_map/ppermute | solution.py:386
  49.1 4.8 %collective-permute-start.3 = (f32[1,512]{1,0:T(1,128)S(1)}, f32[1,512]{1,0:T(1,128)S(1)}, u32[]{:S(2)}, u32[]{:S(2)}) collective-permute-start(f32[1,512]{1,0:T(1,128)S(1)} %add.9), channel_id=1, source_target_pairs={{0,18},{1,19},{2,16},{3,17},{4,22},{5,23},{6,20},{7,21},{8,26},{9,... | collective-permute-start | bytes 6152 | tf_op jit(solution)/shard_map/ppermute | solution.py:387
  53.9 3.6 %collective-permute-start.4 = (f32[1,512]{1,0:T(1,128)S(1)}, f32[1,512]{1,0:T(1,128)S(1)}, u32[]{:S(2)}, u32[]{:S(2)}) collective-permute-start(f32[1,512]{1,0:T(1,128)S(1)} %add.10), channel_id=1, source_target_pairs={{0,16},{4,20},{8,24},{12,28},{16,0},{20,4},{24,8},{28,12},{32,48},... | collective-permute-start | bytes 6152 | tf_op jit(solution)/shard_map/ppermute | solution.py:388

commit v6 on v5

--- a/solution.py
+++ b/solution.py
@@ -44,12 +44,13 @@
     ]
     for copy in copies:
         copy.start()
-    for copy in copies[:3]:
+    for copy in copies[:2]:
         copy.wait()
     for which, out_ref in sides:
         out_ref[antennas:] = jnp.full((8, out_ref.shape[1]), noise[which], F32)
         for k in range(samples.shape[1] // 8):
             out_ref[antennas:, k * TILE : k * TILE + antennas] = samples[which, 8 * k : 8 * k + 8]
+    copies[2].wait()
     give_ref[antennas : antennas + 1, order_lanes(antennas, order_ref.shape[1])] = kept_ref[...].astype(F32)
     for copy in copies[3:]:
         copy.wait()
@@ -157,7 +158,7 @@
     bound, steps = first, jnp.zeros((1, 1), F32)
     for _ in range(10):
         bound = after(bound)
-        steps = steps + jnp.where(bound > 0.0125, 1.0, 0.0)
+        steps = steps + jnp.where(bound > 0.0165, 1.0, 0.0)
     steps = jnp.max(steps).astype(jnp.int32)
 
     def step(index, bound):
@@ -187,7 +188,7 @@
         diag = diag + jnp.sum(own + (e[rows].astype(F32) + twice) * update, axis=0, keepdims=True)
         size = size + jnp.sum(twice * twice, axis=0, keepdims=True)
     diag_ref[...] = diag
-    good = jnp.sum(size) < 3e-5
+    good = jnp.sum(size) < 6e-5
     flag_ref[0] = good.astype(jnp.int32)
 
     @pl.when(jnp.logical_not(good))

time: 58.5 us -> 58.5 us (level)
  no operation moved by 1% of the time
where the time goes in v6:
time: 58.5 us; the launch traced here: 58.3 us
  blocking collectives  33 us (56%)
  waiting for transfers between devices  10.7 us (18%)
  Pallas kernels  8.08 us (14%)
  starting transfers between devices  5.54 us (9%)
  between operations  0.73 us (1%)
    all_to_all x2, blocking collectives, shards(): lax.all_to_all(part, 'stripe', 0, 0, axis_index_groups=planes, tiled=True)  33 us
    pallas_call x1, Pallas kernels, shards(): call(functools.partial(invert, symbols), (struct(1, n), jax.ShapeDtypeStr...  3.74 us
    ppermute x1, waiting for transfers between devices, shards(): diag = diag + lax.ppermute(diag, 'stripe', swap)  3.58 us
    ppermute x1, waiting for transfers between devices, shards(): take = lax.ppermute(give, 'stripe', swap)  3.38 us
    ppermute x1, waiting for transfers between devices, shards(): diag = diag + lax.ppermute(diag, ('stripe', 'sub'), across)  2.62 us
    ppermute x1, starting transfers between devices, shards(): diag = diag + lax.ppermute(diag, ('stripe', 'sub'), across)  2.17 us
    ppermute x1, starting transfers between devices, shards(): take = lax.ppermute(give, 'stripe', swap)  1.77 us
    ppermute x1, starting transfers between devices, shards(): other = lax.ppermute(claimed, 'stripe', swap)  1.59 us
  transfers between devices with their start and end apart: 5, of which 4 were waited for; matrix products, arithmetic and copies ran while one was open for 0% of the time, Pallas kernels for 1%

profile of v6, /device:TPU:0, one launch (start us, length us, event | category | flops | bytes accessed | tf_op | source)
XLA Modules:
  0.0 58.3 jit_solution(14446978883571889962)
XLA Ops:
  0.6 1.0 %shard_map.68 = (f32[72,512]{1,0:T(8,128)S(1)}, f32[72,512]{1,0:T(8,128)S(1)}, s32[1,16]{1,0:T(1,128)S(1)}) custom-call(f32[2,64,512]{2,1,0:T(8,128)} %bitcast.15, f32[2,32,64]{2,1,0:T(8,128)} %received_ref.1, f32[2]{0:T(128)} %bitcast.19, s32[1,16]{1,0:T(1,128)} %bitcast.20), custom_call_target="tpu_custom_call" | custom-call | tf_op jit(solution)/shard_map/pallas_call | solution.py:350
  1.7 1.8 %collective-permute-start = (f32[72,512]{1,0:T(8,128)S(1)}, f32[72,512]{1,0:T(8,128)S(1)}, u32[]{:S(2)}, u32[]{:S(2)}) collective-permute-start(f32[72,512]{1,0:T(8,128)S(1)} %get-tuple-element.14), channel_id=1, source_target_pairs={{0,16},{4,20},{8,24},{12,28},{16,0},{20,4},{24,8},{28,12},{32,48},... | collective-permute-start | bytes 442376 | tf_op jit(solution)/shard_map/ppermute | solution.py:360
  3.5 0.5 shard_map.69.rest_0_
  3.9 3.4 %collective-permute-done.block_ref.take_ref = f32[72,512]{1,0:T(8,128)S(1)} collective-permute-done((f32[72,512]{1,0:T(8,128)S(1)}, f32[72,512]{1,0:T(8,128)S(1)}, u32[]{:S(2)}, u32[]{:S(2)}) %collective-permute-start) | collective-permute-done | bytes 147488 | tf_op jit(solution)/shard_map/ppermute | solution.py:360
  7.3 0.5 shard_map.70
  7.8 19.3 %all_to_all.10 = f32[1168,1,128]{2,1,0:T(1,128)S(1)} all-to-all(f32[1168,1,128]{2,1,0:T(1,128)S(1)} %bitcast.14), channel_id=1, replica_groups={{0,4,8,12,32,36,40,44,64,68,72,76,96,100,104,108},{16,20,24,28,48,52,56..., dimensions={0} | all-to-all | bytes 1196032 | tf_op jit(solution)/shard_map/all_to_all | solution.py:364
  27.2 13.7 %all_to_all.11 = f32[1168,1,128]{2,1,0:T(1,128)S(1)} all-to-all(f32[1168,1,128]{2,1,0:T(1,128)S(1)} %bitcast.18), channel_id=1, replica_groups={{0,4,8,12,32,36,40,44,64,68,72,76,96,100,104,108},{16,20,24,28,48,52,56..., dimensions={0} | all-to-all | bytes 1196032 | tf_op jit(solution)/shard_map/all_to_all | solution.py:369
  41.0 0.0 copy-start.1
  41.0 3.7 %shard_map.71 = (f32[1,512]{1,0:T(1,128)S(1)}, s32[1]{0:T(128)}, bf16[512,512]{1,0:T(8,128)(2,1)S(1)}, bf16[512,512]{1,0:T(8,128)(2,1)S(1)}, bf16[512,512]{1,0:T(8,128)(2,1)S(1)}) custom-call(f32[1168,128]{1,0:T(8,128)S(1)} %bitcast.12), custom_call_target="tpu_custom_call" | custom-call | tf_op jit(solution)/shard_map/pallas_call | solution.py:372
  44.7 0.0 copy-done.1
  44.7 1.2 %shard_map.72.rows_ref.own_ref = f32[64,512]{1,0:T(8,128)S(1)} custom-call(s32[1]{0:T(128)} %get-tuple-element.16.flag_ref, f32[1168,128]{1,0:T(8,128)S(1)} %bitcast.13, f32[2,32,512]{2,1,0:T(8,128)S(1)} %copy-done.1, bf16[512,512]{1,0:T(8,128)(2,1)S(1)} %get-tuple-element.17.x_ref, bf16[512,512]{1,0:T(8,128)(2,1)S(1)} %get-tuple-element.18.e_ref, ...), custom_call_target="tpu_custom_call" | custom-call | flops 1000000000 | bytes 2097152 | tf_op jit(solution)/shard_map/pallas_call | solution.py:379
  46.0 0.0 copy-start
  46.0 0.3 shard_map.73
  46.3 1.6 %collective-permute-start.1 = (f32[40,512]{1,0:T(8,128)S(1)}, f32[40,512]{1,0:T(8,128)S(1)}, u32[]{:S(2)}, u32[]{:S(2)}) collective-permute-start(f32[40,512]{1,0:T(8,128)S(1)} %get-tuple-element.21), channel_id=1, source_target_pairs={{0,16},{4,20},{8,24},{12,28},{16,0},{20,4},{24,8},{28,12},{32,48},... | collective-permute-start | bytes 245768 | tf_op jit(solution)/shard_map/ppermute | solution.py:386
  47.9 0.0 collective-permute-start.2
  47.9 1.2 %collective-permute-done.2 = f32[1,512]{1,0:T(1,128)S(1)} collective-permute-done((f32[1,512]{1,0:T(1,128)S(1)}, f32[1,512]{1,0:T(1,128)S(1)}, u32[]{:S(2)}, u32[]{:S(2)}) %collective-permute-start.2) | collective-permute-done | bytes 2080 | tf_op jit(solution)/shard_map/ppermute | solution.py:387
  49.1 2.2 %collective-permute-start.3 = (f32[1,512]{1,0:T(1,128)S(1)}, f32[1,512]{1,0:T(1,128)S(1)}, u32[]{:S(2)}, u32[]{:S(2)}) collective-permute-start(f32[1,512]{1,0:T(1,128)S(1)} %add.9), channel_id=1, source_target_pairs={{0,18},{1,19},{2,16},{3,17},{4,22},{5,23},{6,20},{7,21},{8,26},{9,... | collective-permute-start | bytes 6152 | tf_op jit(solution)/shard_map/ppermute | solution.py:388
  51.2 2.6 %collective-permute-done.3 = f32[1,512]{1,0:T(1,128)S(1)} collective-permute-done((f32[1,512]{1,0:T(1,128)S(1)}, f32[1,512]{1,0:T(1,128)S(1)}, u32[]{:S(2)}, u32[]{:S(2)}) %collective-permute-start.3) | collective-permute-done | bytes 2080 | tf_op jit(solution)/shard_map/ppermute | solution.py:388
  53.9 0.0 collective-permute-start.4
  53.9 3.6 %collective-permute-done.4 = f32[1,512]{1,0:T(1,128)S(1)} collective-permute-done((f32[1,512]{1,0:T(1,128)S(1)}, f32[1,512]{1,0:T(1,128)S(1)}, u32[]{:S(2)}, u32[]{:S(2)}) %collective-permute-start.4) | collective-permute-done | bytes 2080 | tf_op jit(solution)/shard_map/ppermute | solution.py:389
  57.4 0.0 collective-permute-done.1.other_ref
  57.4 0.0 copy-done
  57.5 0.8 %shard_map.74 = (f32[2,32,64]{2,1,0:T(8,128)}, f32[2,16,32]{2,1,0:T(8,128)}) custom-call(f32[64,512]{1,0:T(8,128)S(1)} %shard_map.72.rows_ref.own_ref, f32[40,512]{1,0:T(8,128)S(1)} %collective-permute-done.1.other_ref, f32[16,32]{1,0:T(8,128)S(1)} %get-tuple-element.22.mine_ref, f32[1,512]{1,0:T(1,128)S(1)} %add.11.diag_ref, f32[2,64,512]{2,1,0:T(8,128)S(1)} %bitcast.16), custom_call_target="tpu_custom_call" | custom-call | tf_op jit(solution)/shard_map/pallas_call | solution.py:390
  (7 shorter events, 0.2 us)
Async XLA Ops:
  1.7 5.6 %collective-permute-start = (f32[72,512]{1,0:T(8,128)S(1)}, f32[72,512]{1,0:T(8,128)S(1)}, u32[]{:S(2)}, u32[]{:S(2)}) collective-permute-start(f32[72,512]{1,0:T(8,128)S(1)} %get-tuple-element.14), channel_id=1, source_target_pairs={{0,16},{4,20},{8,24},{12,28},{16,0},{20,4},{24,8},{28,12},{32,48},... | collective-permute-start | bytes 442376 | tf_op jit(solution)/shard_map/ppermute | solution.py:360
  41.0 3.8 %copy-start.1 = (f32[2,32,512]{2,1,0:T(8,128)S(1)}, f32[2,32,512]{2,1,0:T(8,128)}, u32[]{:S(2)}) copy-start(f32[2,32,512]{2,1,0:T(8,128)} %downlink_ref.1) | copy-start | bytes 393220
  46.0 11.5 %copy-start = (f32[2,1,64,512]{3,2,1,0:T(8,128)S(1)}, f32[2,1,64,512]{3,2,1,0:T(8,128)}, u32[]{:S(2)}) copy-start(f32[2,1,64,512]{3,2,1,0:T(8,128)} %param.5) | copy-start | bytes 786436
  46.3 11.2 %collective-permute-start.1 = (f32[40,512]{1,0:T(8,128)S(1)}, f32[40,512]{1,0:T(8,128)S(1)}, u32[]{:S(2)}, u32[]{:S(2)}) collective-permute-start(f32[40,512]{1,0:T(8,128)S(1)} %get-tuple-element.21), channel_id=1, source_target_pairs={{0,16},{4,20},{8,24},{12,28},{16,0},{20,4},{24,8},{28,12},{32,48},... | collective-permute-start | bytes 245768 | tf_op jit(solution)/shard_map/ppermute | solution.py:386
  47.9 1.2 %collective-permute-start.2 = (f32[1,512]{1,0:T(1,128)S(1)}, f32[1,512]{1,0:T(1,128)S(1)}, u32[]{:S(2)}, u32[]{:S(2)}) collective-permute-start(f32[1,512]{1,0:T(1,128)S(1)} %get-tuple-element.23), channel_id=1, source_target_pairs={{0,1},{1,0},{2,3},{3,2},{4,5},{5,4},{6,7},{7,6},{8,9},{9,8},{10,11... | collective-permute-start | bytes 6152 | tf_op jit(solution)/shard_map/ppermute | solution.py:387
  49.1 4.8 %collective-permute-start.3 = (f32[1,512]{1,0:T(1,128)S(1)}, f32[1,512]{1,0:T(1,128)S(1)}, u32[]{:S(2)}, u32[]{:S(2)}) collective-permute-start(f32[1,512]{1,0:T(1,128)S(1)} %add.9), channel_id=1, source_target_pairs={{0,18},{1,19},{2,16},{3,17},{4,22},{5,23},{6,20},{7,21},{8,26},{9,... | collective-permute-start | bytes 6152 | tf_op jit(solution)/shard_map/ppermute | solution.py:388
  53.9 3.6 %collective-permute-start.4 = (f32[1,512]{1,0:T(1,128)S(1)}, f32[1,512]{1,0:T(1,128)S(1)}, u32[]{:S(2)}, u32[]{:S(2)}) collective-permute-start(f32[1,512]{1,0:T(1,128)S(1)} %add.10), channel_id=1, source_target_pairs={{0,16},{4,20},{8,24},{12,28},{16,0},{20,4},{24,8},{28,12},{32,48},... | collective-permute-start | bytes 6152 | tf_op jit(solution)/shard_map/ppermute | solution.py:389
